TPU v7x, 32 devices: a whole 2x2x4 slice. The times are simulated.
32 devices in a mesh: span: 8 (over z, x), plane: 4 (over y, core).
Axes of the slice: x: 2, y: 2, z: 4, core: 2. Of those that a mesh axis runs over, the one named last changes fastest.
Arguments:
- velocity: float32 [3, 1024, 512, 128], P(None, 'span', 'plane'), may hold values from -6 to 6
- wall_history: float32 [255, 1024, 512], P(None, 'span', 'plane'), may hold values from -6 to 6
- phase_bin: int32 [256], replicated, may hold values from 0 to 63
- station_of: int32 [1024], P('span'), may hold values from 0 to 31
- wall_index: int32 [512], P('plane'), may hold values from 0 to 7
Outputs:
- corrected: float32 [3, 1024, 512, 128], P(None, 'span', 'plane')
- pressure: float32 [1024, 512, 128], P('span', 'plane')
- coefficients: float32 [32, 8192], P('span')
All inputs are finite; a program needn't handle non-finite values.
Results may differ from a plain program's by a relative error of at most 0.000078.
Values sent between devices are 32-bit elements; how exact they have to be, the bound alone decides.
No kernel may reach another device: no remote copies, remote signals or barrier semaphores. Data moves between devices by JAX's collectives and lax.ppermute only.
A program may use at most 192 MiB of HBM per device.

v0:
```python
import math

import jax
import jax.numpy as jnp
from jax import lax
from jax.sharding import PartitionSpec as P

NZ = 1024
NA = 128
NF = 64
NBIN = 64
ITERS = 4
WALL_SPAN = 8
ST_DEV = 4


PRECISE = lax.Precision.HIGHEST


def with_halo(block, sides, width):
    for axis, dim in sides:
        count = lax.axis_size(axis)
        forward = [(i, i + 1) for i in range(count - 1)]
        forward.append((count - 1, 0))
        backward = [(target, source) for source, target in forward]
        low = lax.ppermute(
            lax.slice_in_dim(block, block.shape[dim] - width, None, axis=dim), axis, forward
        )
        high = lax.ppermute(lax.slice_in_dim(block, 0, width, axis=dim), axis, backward)
        block = jnp.concatenate([low, block, high], axis=dim)
    return block


def radial_diff(field):
    padded = jnp.pad(field, ((0, 0), (0, 0), (1, 1)))
    return padded[..., 2:] - padded[..., :-2]


def radial_pair(field):
    padded = jnp.pad(field, ((0, 0), (0, 0), (1, 1)))
    return padded[..., :-2] + padded[..., 2:]


def mode_diagonal(modes):
    angle = 2.0 * math.pi / NZ * modes.astype(jnp.float32)
    return 6.0 - 2.0 * jnp.cos(angle)


def azimuth_basis(first_cell, cells, total):
    column = jnp.arange(NA)
    upper = column >= NA // 2
    harmonic = jnp.where(upper, column - NA // 2 + 1, column)
    index = first_cell + jnp.arange(cells)
    phase = index[:, None] * harmonic[None, :] % total
    angle = 2.0 * math.pi / total * phase.astype(jnp.float32)
    return jnp.where(upper[None, :], jnp.sin(angle), jnp.cos(angle))


def phase_weights(phase_bin, scale):
    column = jnp.arange(NF)
    upper = column >= NF // 2
    harmonic = jnp.where(upper, column - NF // 2 + 1, column)
    phase = phase_bin[:, None] * harmonic[None, :] % NBIN
    angle = 2.0 * math.pi / NBIN * phase.astype(jnp.float32)
    return jnp.where(upper[None, :], jnp.sin(angle), jnp.cos(angle)) * scale


def cas_matrix():
    row_index = jnp.arange(NZ)
    phase = row_index[:, None] * row_index[None, :] % NZ
    angle = 2.0 * math.pi / NZ * phase.astype(jnp.float32)
    return jnp.cos(angle) + jnp.sin(angle)


def local(velocity, wall_history, phase_bin, station_of, wall_index):
    span_cells = velocity.shape[1]
    theta_cells = velocity.shape[2]
    plane_count = lax.axis_size("plane")
    total_theta = theta_cells * plane_count
    extended = with_halo(velocity[1:], (("span", 1), ("plane", 2)), 1)
    divergence = (
        0.5 * radial_diff(velocity[0])
        + 0.5 * (extended[0, 1:-1, 2:, :] - extended[0, 1:-1, :-2, :])
        + 0.5 * (extended[1, 2:, 1:-1, :] - extended[1, :-2, 1:-1, :])
    )
    source = -divergence
    cas_table = cas_matrix()

    def forward(pencil):
        width = pencil.shape[1]
        depth = pencil.shape[2]
        product = jnp.dot(
            cas_table, pencil.reshape(NZ, -1), precision=PRECISE, preferred_element_type=jnp.float32
        )
        return product.reshape(NZ, width, depth)

    spectra_lines = forward(lax.all_to_all(source, "span", split_axis=1, concat_axis=0, tiled=True))
    spectra = lax.all_to_all(spectra_lines, "span", split_axis=0, concat_axis=1, tiled=True)
    modes_global = lax.axis_index("span") * span_cells + jnp.arange(span_cells)
    diagonal = mode_diagonal(modes_global)[:, None, None]
    potential = spectra / diagonal
    for sweep in range(ITERS):
        padded = with_halo(potential, (("plane", 1),), 1)
        potential = (
            spectra + padded[:, :-2, :] + padded[:, 2:, :] + radial_pair(potential)
        ) / diagonal
    pencil = lax.all_to_all(potential, "span", split_axis=1, concat_axis=0, tiled=True)
    width = pencil.shape[1]
    depth = pencil.shape[2]
    product = jnp.dot(
        cas_table, pencil.reshape(NZ, -1), precision=PRECISE, preferred_element_type=jnp.float32
    )
    pressure_lines = product.reshape(NZ, width, depth) / NZ
    pressure = lax.all_to_all(pressure_lines, "span", split_axis=0, concat_axis=1, tiled=True)
    pressure_ext = with_halo(pressure, (("span", 0), ("plane", 1)), 1)
    gradient = jnp.stack(
        [
            0.5 * radial_diff(pressure),
            0.5 * (pressure_ext[1:-1, 2:, :] - pressure_ext[1:-1, :-2, :]),
            0.5 * (pressure_ext[2:, 1:-1, :] - pressure_ext[:-2, 1:-1, :]),
        ]
    )
    corrected = velocity - gradient
    wall_select = (wall_index[:, None] == jnp.arange(WALL_SPAN)[None, :]).astype(jnp.float32)
    wall_pressure = jnp.sum(pressure[:, :, :WALL_SPAN] * wall_select[None, :, :], axis=2)
    samples = jnp.concatenate([wall_history, wall_pressure[None]], axis=0)
    sample_count = samples.shape[0]
    basis = azimuth_basis(lax.axis_index("plane") * theta_cells, theta_cells, total_theta)
    amplitudes = jnp.dot(
        samples.reshape(-1, theta_cells),
        basis,
        precision=PRECISE,
        preferred_element_type=jnp.float32,
    ).reshape(sample_count, span_cells, NA)
    weights = phase_weights(phase_bin, 1.0 / math.sqrt(total_theta * sample_count))
    by_plane = jnp.einsum("tza,tf->zaf", amplitudes, weights, precision=PRECISE).reshape(
        span_cells, NA * NF
    )
    targets = jnp.arange(ST_DEV * lax.axis_size("span"))
    selector = (station_of[:, None] == targets[None, :]).astype(jnp.float32)
    partial_rows = lax.psum_scatter(
        jnp.dot(selector.T, by_plane, precision=PRECISE, preferred_element_type=jnp.float32),
        "span",
        scatter_dimension=0,
        tiled=True,
    )
    coefficients = lax.psum(partial_rows, "plane")
    return (corrected, pressure, coefficients)


def solution(mesh):
    in_specs = (
        P(None, "span", "plane", None),
        P(None, "span", "plane"),
        P(),
        P("span"),
        P("plane"),
    )
    out_specs = (P(None, "span", "plane", None), P("span", "plane", None), P("span", None))
    return jax.shard_map(local, mesh=mesh, in_specs=in_specs, out_specs=out_specs, check_vma=False)
```

profile of v0, /device:TPU:0, one launch (start us, length us, event | category | flops | bytes accessed | tf_op | source)
XLA Modules:
  0.0 1269.0 jit_solution(15156536948828249830)
XLA Ops:
  7.2 1.0 fusion.117
  8.2 3.0 collective-permute-start
  11.2 3.1 collective-permute-start.1
  14.3 24.9 %copy.78 = f32[3,128,128,128]{3,1,2,0:T(8,128)} copy(f32[3,128,128,128]{3,2,1,0:T(8,128)} %param.5) | data formatting | bytes 50331648 | tf_op args[0]
  39.1 6.6 slice.215
  45.7 0.7 collective-permute-start.2
  46.5 7.9 slice_bitcast_fusion
  54.4 15.3 %fusion.8 = f32[128,128,128]{2,0,1:T(8,128)} fusion(f32[128,128,128]{2,0,1:T(8,128)} %slice_bitcast_fusion, f32[2,128,128,128]{3,1,2,0:T(8,128)S(1)} %slice.215, f32[2,1,128,128]{3,1,2,0:T(1,128)S(1)} %collective-permute-done, f32[2,1,128,128]{3,1,2,0:T(1,128)S(1)} %collective-permute-done.1, f32[2,130,1,128]{3,1,2,0:T(8,128)S(1)} %collective-permute-done.3, ...), kind=kLoop, calls=%fused_computation.21 | loop fusion | flops 31457280 | bytes 34082816 | tf_op jit(solution)/shard_map/neg | solution.py:86
  69.7 190.0 %all_to_all.66 = f32[128,128,128]{2,0,1:T(8,128)} all-to-all(f32[128,128,128]{2,0,1:T(8,128)} %fusion.8), channel_id=1, replica_groups=mesh['span'=8,'plane'=4] {'span'}, dimensions={1} | all-to-all | bytes 16777216 | tf_op jit(solution)/shard_map/all_to_all | solution.py:97
  259.7 9.3 copy.68
  268.9 5.5 copy.93
  274.4 52.7 %fusion.48 = f32[1024,16,128]{2,0,1:T(8,128)S(1)} fusion(f32[16,128,1024]{2,1,0:T(8,128)S(1)} %bitcast.98), kind=kOutput, calls=%fused_computation.94 | convolution fusion | flops 25785532416 | bytes 16777216 | tf_op jit(solution)/shard_map/dot_general | solution.py:92
  327.1 8.3 copy.69
  335.3 5.0 all-to-all-start.1
  340.4 183.6 %all-to-all-done.1 = f32[1024,16,128]{2,1,0:T(8,128)} async-done(((f32[1024,16,128]{2,1,0:T(8,128)}), f32[1024,16,128]{2,1,0:T(8,128)}, u32[]{:S(2)}, u32[]{:S(2)}) %all-to-all-start.1) | async-done | bytes 8388640 | tf_op jit(solution)/shard_map/all_to_all | solution.py:98
  523.9 4.4 copy.70
  528.3 1.4 bitcast_divide_fusion
  529.9 1.7 collective-permute-start.5
  531.6 1.9 collective-permute-done.4
  533.6 15.6 %fusion.11 = f32[128,128,128]{2,1,0:T(8,128)S(1)} fusion(f32[128,128,128]{2,1,0:T(8,128)} %copy-done.1, f32[128,1,128]{2,1,0:T(1,128)S(1)} %collective-permute-done.5, f32[128,1,128]{2,1,0:T(1,128)S(1)} %collective-permute-done.4, f32[128,8,16,128]{3,2,1,0:T(8,128)S(1)} %copy.70, f32[128]{0:T(128)S(1)} %multiply_subtract_fusion), kind=kLoop, calls=%fused_computation.24 | loop fusion | flops 14680064 | bytes 25297408 | tf_op jit(solution)/shard_map/div | solution.py:104
  549.3 1.2 collective-permute-start.6
  550.5 0.7 collective-permute-start.7
  551.2 1.9 collective-permute-done.6
  553.1 8.2 fusion.14
  561.2 1.3 fusion.120
  562.5 1.2 collective-permute-start.8
  563.8 0.7 collective-permute-start.9
  564.4 1.9 collective-permute-done.8
  566.3 15.8 %fusion.17 = f32[128,128,128]{2,1,0:T(8,128)S(1)} fusion(f32[128,128,128]{2,1,0:T(8,128)} %fusion.14, f32[128,1,128]{2,1,0:T(1,128)S(1)} %collective-permute-done.9, f32[128,1,128]{2,1,0:T(1,128)S(1)} %collective-permute-done.8, f32[128,8,16,128]{3,2,1,0:T(8,128)S(1)} %copy.70, f32[128]{0:T(128)S(1)} %multiply_subtract_fusion), kind=kLoop, calls=%fused_computation.30 | loop fusion | flops 14680064 | bytes 25297408 | tf_op jit(solution)/shard_map/div | solution.py:104
  582.2 1.2 collective-permute-start.10
  583.5 0.7 collective-permute-start.11
  584.1 1.9 collective-permute-done.10
  586.1 8.2 fusion.20
  594.2 8.2 copy.71
  602.4 188.7 %all_to_all.67 = f32[128,128,128]{2,0,1:T(8,128)S(1)} all-to-all(f32[128,128,128]{2,0,1:T(8,128)S(1)} %copy.71), channel_id=1, replica_groups=mesh['span'=8,'plane'=4] {'span'}, dimensions={1} | all-to-all | bytes 16777216 | tf_op jit(solution)/shard_map/all_to_all | solution.py:107
  791.2 4.7 copy.73
  795.9 7.5 copy.92
  803.4 9.2 copy.74
  812.7 47.9 %broadcast_multiply_fusion = f32[1024,16,128]{2,0,1:T(8,128)S(1)} fusion(f32[16,128,1024]{2,1,0:T(8,128)} %bitcast.99), kind=kOutput, calls=%fused_computation.96 | convolution fusion | flops 25787629568 | bytes 16777216 | tf_op jit(solution)/shard_map/dot_general | solution.py:110
  860.6 8.3 copy.75
  868.9 5.0 all-to-all-start.3
  873.9 17.8 %copy.80 = f32[255,128,128]{2,0,1:T(8,128)} copy(f32[255,128,128]{2,1,0:T(8,128)} %param.6) | data formatting | bytes 33423360 | tf_op args[1]
  891.7 0.6 dynamic-slice
  893.1 164.3 %all-to-all-done.3 = f32[1024,16,128]{2,1,0:T(8,128)} async-done(((f32[1024,16,128]{2,1,0:T(8,128)}), f32[1024,16,128]{2,1,0:T(8,128)}, u32[]{:S(2)}, u32[]{:S(2)}) %all-to-all-start.3) | async-done | bytes 8388640 | tf_op jit(solution)/shard_map/all_to_all | solution.py:114
  1057.4 4.4 copy.94
  1061.8 1.5 collective-permute-start.12
  1063.4 3.2 collective-permute-start.13
  1066.6 5.9 copy.77
  1072.5 3.3 copy-done
  1075.8 2.3 fusion.24
  1078.1 20.2 %fusion = f32[256,128,128]{2,0,1:T(8,128)S(1)} fusion(f32[1,128,128]{2,0,1:T(1,128)S(1)} %bitcast.100, f32[255,128,128]{2,0,1:T(8,128)} %copy.80, s32[128]{0:T(128)S(1)} %get-tuple-element.31, s32[128]{0:T(128)S(1)} %get-tuple-element.32, pred[128]{0:T(512)(128)(4,1)S(1)} %iota_compare_fusion.3), kind=kOutput, calls=%fused_computation.13 | convolution fusion | flops 6446891008 | bytes 33555584 | tf_op jit(solution)/shard_map/dot_general | solution.py:129
  1098.4 13.0 %fusion.61 = f32[128,128,64]{1,2,0:T(8,128)} fusion(f32[256,128,128]{2,0,1:T(8,128)S(1)} %fusion, s32[64]{0:T(128)S(1)} %add_select_fusion.3, s32[256]{0:T(256)S(1)} %copy-done.3, pred[64]{0:T(512)(128)(4,1)S(1)} %iota_compare_fusion.2), kind=kOutput, calls=%fused_computation.123 | convolution fusion | flops 3221487616 | bytes 20972864 | tf_op jit(solution)/shard_map/tza,tf->zaf/dot_general | solution.py:136
  1111.3 5.4 copy.81
  1116.8 1.0 pad_maximum_fusion.29
  1117.9 0.7 collective-permute-start.15
  1118.6 0.4 copy-done.2
  1119.0 3.4 fusion.81
  1122.4 11.6 copy.83
  1134.4 28.6 %fusion.30 = (f32[1,128,128,128]{3,1,2,0:T(8,128)}, f32[1,128,128,128]{3,1,2,0:T(8,128)}, f32[1,128,128,128]{3,1,2,0:T(8,128)}) fusion(f32[130,1,128]{2,0,1:T(8,128)S(1)} %collective-permute-done.15, f32[1,128,128]{2,0,1:T(1,128)S(1)} %collective-permute-done.13, f32[128,128,128]{2,0,1:T(8,128)} %bitcast.90, f32[1,128,128]{2,0,1:T(1,128)S(1)} %collective-permute-done.12, ...), kind=kLoop, calls=%fused_computation.49 | loop fusion | flops 29360128 | bytes 33818624 | tf_op jit(solution)/shard_map/stack | solution.py:116
  1163.0 45.9 %all-reduce.12.cloned.1.call-done = f32[32,8192]{1,0:T(8,128)} async-done(((f32[32,8192]{1,0:T(8,128)}), f32[32,8192]{1,0:T(8,128)}) %all-reduce.12.cloned.1.call-update) | async-done | bytes 1048592
  1208.9 1.6 constant_dynamic-slice_fusion
  1210.6 20.5 %maximum_subtract_fusion = f32[3,128,128,128]{3,1,2,0:T(8,128)S(1)} fusion(f32[1,128,128,128]{3,1,2,0:T(8,128)} %get-tuple-element.17, f32[1,128,128,128]{3,1,2,0:T(8,128)} %get-tuple-element.16, f32[1,128,128,128]{3,1,2,0:T(8,128)} %get-tuple-element.20, f32[3,128,128,128]{3,2,1,0:T(8,128)} %param.5), kind=kLoop, calls=%fused_computation | loop fusion | flops 18874368 | bytes 75497472 | tf_op jit(solution)/shard_map/sub | solution.py:123
  1231.1 29.1 %copy.82 = f32[3,128,128,128]{3,2,1,0:T(8,128)} copy(f32[3,128,128,128]{3,1,2,0:T(8,128)S(1)} %maximum_subtract_fusion) | data formatting | bytes 50331648
  1260.2 1.6 copy.97
  (44 shorter events, 1.2 us)
Async XLA Ops:
  8.2 37.5 %collective-permute-start = (f32[2,1,128,128]{3,1,2,0:T(1,128)S(1)}, f32[2,1,128,128]{3,1,2,0:T(1,128)S(1)}, u32[]{:S(2)}, u32[]{:S(2)}) collective-permute-start(f32[2,1,128,128]{3,1,2,0:T(1,128)S(1)} %bitcast.102), channel_id=1, source_target_pairs={{0,4},{4,8},{8,12},{12,16},{16,20},{20,24},{24,28},{28,0},{1,5},{5... | collective-permute-start | bytes 393224 | tf_op jit(solution)/shard_map/ppermute | solution.py:26
  11.2 34.5 %collective-permute-start.1 = (f32[2,1,128,128]{3,1,2,0:T(1,128)S(1)}, f32[2,1,128,128]{3,1,2,0:T(1,128)S(1)}, u32[]{:S(2)}, u32[]{:S(2)}) collective-permute-start(f32[2,1,128,128]{3,1,2,0:T(1,128)S(1)} %bitcast.101), channel_id=1, source_target_pairs={{4,0},{8,4},{12,8},{16,12},{20,16},{24,20},{28,24},{0,28},{5,1},{9... | collective-permute-start | bytes 393224 | tf_op jit(solution)/shard_map/ppermute | solution.py:29
  45.7 8.6 collective-permute-start.2
  46.5 7.9 collective-permute-start.3
  335.3 188.6 %all-to-all-start.1 = ((f32[1024,16,128]{2,1,0:T(8,128)}), f32[1024,16,128]{2,1,0:T(8,128)}, u32[]{:S(2)}, u32[]{:S(2)}) async-start(f32[1024,16,128]{2,1,0:T(8,128)} %copy.69), calls=%async_computation.1 | async-start | bytes 16777216 | tf_op jit(solution)/shard_map/all_to_all | solution.py:98
  529.7 3.9 copy-start.1
  529.8 3.7 collective-permute-start.4
  529.9 3.7 collective-permute-start.5
  549.3 3.7 collective-permute-start.6
  550.5 2.6 collective-permute-start.7
  562.5 3.8 collective-permute-start.8
  563.8 2.6 collective-permute-start.9
  582.2 3.8 collective-permute-start.10
  583.5 2.6 collective-permute-start.11
  868.9 188.5 %all-to-all-start.3 = ((f32[1024,16,128]{2,1,0:T(8,128)}), f32[1024,16,128]{2,1,0:T(8,128)}, u32[]{:S(2)}, u32[]{:S(2)}) async-start(f32[1024,16,128]{2,1,0:T(8,128)} %copy.75), calls=%async_computation.3 | async-start | bytes 16777216 | tf_op jit(solution)/shard_map/all_to_all | solution.py:114
  873.8 335.1 %all-reduce.12.cloned.1.call-start = ((), (), s32[]{:S(2)}) async-start(), calls=%async_computation.5 | async-start | bytes 2097152
  873.9 17.8 %copy-start.6 = (u32[32]{0:T(128)S(1)}, u32[32]{0:T(128)}, u32[]{:S(2)}) copy-start(u32[32]{0:T(128)} %constant.101) | copy-start | bytes 388
  873.9 19.1 %copy-start.4 = (s32[128]{0:T(128)S(1)}, s32[128]{0:T(128)}, u32[]{:S(2)}) copy-start(s32[128]{0:T(128)} %param.9) | copy-start | bytes 1540
  1061.8 54.9 %collective-permute-start.12 = (f32[1,128,128]{2,0,1:T(1,128)S(1)}, f32[1,128,128]{2,0,1:T(1,128)S(1)}, u32[]{:S(2)}, u32[]{:S(2)}) collective-permute-start(f32[1,128,128]{2,0,1:T(1,128)S(1)} %bitcast.104), channel_id=1, source_target_pairs={{0,4},{4,8},{8,12},{12,16},{16,20},{20,24},{24,28},{28,0},{1,5},{5... | collective-permute-start | bytes 196616 | tf_op jit(solution)/shard_map/ppermute | solution.py:26
  1063.4 53.4 %collective-permute-start.13 = (f32[1,128,128]{2,0,1:T(1,128)S(1)}, f32[1,128,128]{2,0,1:T(1,128)S(1)}, u32[]{:S(2)}, u32[]{:S(2)}) collective-permute-start(f32[1,128,128]{2,0,1:T(1,128)S(1)} %bitcast.103), channel_id=1, source_target_pairs={{4,0},{8,4},{12,8},{16,12},{20,16},{24,20},{28,24},{0,28},{5,1},{9... | collective-permute-start | bytes 196616 | tf_op jit(solution)/shard_map/ppermute | solution.py:29
  1072.5 3.3 copy-start
  1078.1 20.2 %copy-start.3 = (s32[256]{0:T(256)S(1)}, s32[256]{0:T(256)}, u32[]{:S(2)}) copy-start(s32[256]{0:T(256)} %param.7) | copy-start | bytes 3076
  1111.3 7.2 copy-start.5
  1116.8 2.2 copy-start.2
  1117.8 16.6 %collective-permute-start.14 = (f32[130,1,128]{2,0,1:T(8,128)S(1)}, f32[130,1,128]{2,0,1:T(8,128)S(1)}, u32[]{:S(2)}, u32[]{:S(2)}) collective-permute-start(f32[130,1,128]{2,0,1:T(8,128)S(1)} %get-tuple-element.18), channel_id=1, source_target_pairs={{1,0},{2,1},{3,2},{0,3},{5,4},{6,5},{7,6},{4,7},{9,8},{10,9},{11,1... | collective-permute-start | bytes 199688 | tf_op jit(solution)/shard_map/ppermute | solution.py:29
  1117.9 16.5 %collective-permute-start.15 = (f32[130,1,128]{2,0,1:T(8,128)S(1)}, f32[130,1,128]{2,0,1:T(8,128)S(1)}, u32[]{:S(2)}, u32[]{:S(2)}) collective-permute-start(f32[130,1,128]{2,0,1:T(8,128)S(1)} %get-tuple-element.19), channel_id=1, source_target_pairs={{0,1},{1,2},{2,3},{3,0},{4,5},{5,6},{6,7},{7,4},{8,9},{9,10},{10,1... | collective-permute-start | bytes 199688 | tf_op jit(solution)/shard_map/ppermute | solution.py:26
  1134.1 126.1 %all-reduce.10.cloned.1.call-start = ((), (), s32[]{:S(2)}) async-start(), calls=%async_computation.4 | async-start | bytes 262144 | tf_op jit(solution)/shard_map/psum | solution.py:147
Sparse Core Ops, SparseCore 0:
  1134.2 74.6 all-reduce.11
  1211.9 30.9 all-reduce.9
where the time goes:
time: 1280 us; the launch traced here: 1270 us
  waiting for transfers between devices  401 us (31%)
  blocking collectives  379 us (30%)
  local copies, waits for them, and re-layouts  189 us (15%)
  matrix products  137 us (11%)
  other arithmetic  117 us (9%)
  starting transfers between devices  30 us (2%)
  between operations  15.5 us (1%)
    all_to_all x1, blocking collectives, local(): lax.all_to_all(source, 'span', split_axis=1, concat_axis=0, tiled=True)  190 us
    all_to_all x1, blocking collectives, local(): lax.all_to_all(potential, 'span', split_axis=1, concat_axis=0, tiled=True)  189 us
    all_to_all x1, waiting for transfers between devices, local(): lax.all_to_all(spectra_lines, 'span', split_axis=0, concat_axis=1, tiled=...  184 us
    all_to_all x1, waiting for transfers between devices, local(): lax.all_to_all(pressure_lines, 'span', split_axis=0, concat_axis=1, tiled...  164 us
    unnamed x23, local copies, waits for them, and re-layouts  104 us
    dot_general x1, matrix products, forward(): jnp.dot(cas_table, pencil.reshape(NZ, -1), precision=PRECISE, preferred_e...  52.7 us
    dot_general x1, matrix products, local(): jnp.dot(cas_table, pencil.reshape(NZ, -1), precision=PRECISE, preferred_e...  47.9 us
    div x4, other arithmetic, local(): (spectra + padded[:, :-2, :] + padded[:, 2:, :] + radial_pair(potential))...  47.7 us
  transfers between devices with their start and end apart: 20, of which 7 were waited for; matrix products, arithmetic and copies ran while one was open for 16% of the time, Pallas kernels for 0%

commit v1 on v0

v1 whole, which is shorter than its diff:
```python
import math

import jax
import jax.numpy as jnp
import numpy as np
from jax import lax
from jax.experimental import pallas as pl
from jax.experimental.pallas import tpu as pltpu
from jax.sharding import PartitionSpec as P

NZ = 1024
NA = 128
NF = 64
NBIN = 64
ITERS = 4
WALL_SPAN = 8
ST_DEV = 4
ORDER = ITERS + 1
TILE = 8
RHO = 3.0 - 2.0 * math.sqrt(2.0)
PRECISE = lax.Precision.HIGHEST


def representable(table):
    table = np.asarray(table, np.float64)
    return np.where(np.abs(table) < np.finfo(np.float32).tiny, 0.0, table).astype(np.float32)


def inverse_entry(distance):
    j = ORDER - 1
    return RHO ** (ORDER + distance) * sum(
        math.comb(j + i, j) * math.comb(j + distance + i, j) * RHO ** (2 * i) for i in range(40)
    )


def carry_weight(node, distance):
    basis = 1.0
    for other in range(ORDER):
        if other != node:
            basis *= (distance - other) / (node - other)
    return RHO ** (distance - node) * basis


def carry_table(cells):
    return representable([[carry_weight(b, d) for d in range(cells)] for b in range(ORDER)])


def hop_table(offset):
    return representable([[carry_weight(b, offset + d) for d in range(-1, ORDER)] for b in range(ORDER)])


def span_rows(cells):
    return cells + 3 * TILE


def solve_table(cells):
    rows = span_rows(cells)
    table = np.zeros((cells + TILE, rows))
    for i in range(cells + 2):
        for z in range(-ORDER - ITERS, cells + ORDER + ITERS):
            table[i, (z + TILE) % rows] = inverse_entry(abs(i - 1 - z))
    return representable(table)


def split(x):
    high = x.astype(jnp.bfloat16)
    low = (x - high.astype(jnp.float32)).astype(jnp.bfloat16)
    return high, low


def lane_pair(x, sign):
    axis = x.ndim - 1
    cells = x.shape[axis]
    lane = lax.broadcasted_iota(jnp.int32, x.shape, axis)
    low = jnp.where(lane == 0, 0.0, pltpu.roll(x, 1, axis))
    high = jnp.where(lane == cells - 1, 0.0, pltpu.roll(x, cells - 1, axis))
    return low + high if sign > 0 else low - high


def source_call(velocity):
    _, s_, t_, r_ = velocity.shape
    wide = t_ + 2 * TILE
    blocks = s_ // TILE
    table = carry_table(s_)
    reach = 1 + max(int(np.max(np.nonzero(row)[0])) for row in table) // TILE
    table = jnp.asarray(table)

    def kernel(tab, v, before, after, s_out, zr, zl, scr):
        c = pl.program_id(0)

        @pl.when(c == 0)
        def _():
            zr[...] = jnp.zeros_like(zr)
            zl[...] = jnp.zeros_like(zl)
            zl[ORDER, TILE : TILE + t_] = -0.5 * v[2, 0]

        @pl.when(c == blocks - 1)
        def _():
            zr[0, TILE : TILE + t_] = 0.5 * v[2, TILE - 1]

        @pl.when(c < blocks)
        def _():
            row = lax.broadcasted_iota(jnp.int32, (t_, r_), 0)
            tile_row = lax.broadcasted_iota(jnp.int32, (TILE, r_), 0)
            for i in range(TILE):
                if i == 0:
                    low = jnp.where(c == 0, 0.0, before[0, 0])
                else:
                    low = v[2, i - 1]
                if i == TILE - 1:
                    high = jnp.where(c == blocks - 1, 0.0, after[0, 0])
                else:
                    high = v[2, i + 1]
                turn = v[1, i]
                left = jnp.where(row == 0, 0.0, pltpu.roll(turn, 1, 0))
                right = jnp.where(row == t_ - 1, 0.0, pltpu.roll(turn, t_ - 1, 0))
                base = i * wide
                scr[base + TILE : base + TILE + t_] = 0.5 * (
                    lane_pair(v[0, i], -1) + (left - right) + (low - high)
                )
                first = pltpu.roll(turn[:TILE], TILE - 1, 0)
                last = pltpu.roll(turn[t_ - TILE :], 1, 0)
                scr[base : base + TILE] = jnp.where(tile_row == TILE - 1, -0.5 * first, 0.0)
                scr[base + TILE + t_ : base + wide] = jnp.where(tile_row == 0, 0.5 * last, 0.0)

            def move(t, _):
                s_out[t] = scr[pl.ds(t, TILE, stride=wide), :]
                return 0

            lax.fori_loop(0, wide, move, 0, unroll=8)

            def carry(out, first, flip):
                def tile(j, _):
                    at = pl.multiple_of(j * TILE, TILE)
                    cells = [scr[pl.ds(i * wide + at, TILE), :] for i in range(TILE)]
                    for b in range(ORDER):
                        total = out[first + (ORDER - 1 - b if flip else b), pl.ds(at, TILE), :]
                        for i in range(TILE):
                            z = c * TILE + i
                            total = total + tab[b, (s_ - 1 - z) if flip else z] * cells[i]
                        out[first + (ORDER - 1 - b if flip else b), pl.ds(at, TILE), :] = total
                    return 0

                lax.fori_loop(0, wide // TILE, tile, 0)

            @pl.when(c >= blocks - reach)
            def _():
                carry(zr, 1, True)

            @pl.when(c < reach)
            def _():
                carry(zl, 0, False)

        @pl.when(c == blocks)
        def _():
            s_out[...] = jnp.zeros_like(s_out)
            s_out[:, 0, :] = zr[0]
            s_out[:, TILE - 1, :] = zl[ORDER]

    return pl.pallas_call(
        kernel,
        grid=(blocks + 1,),
        in_specs=[
            pl.BlockSpec(memory_space=pltpu.SMEM),
            pl.BlockSpec((3, TILE, t_, r_), lambda c: (0, jnp.minimum(c, blocks - 1), 0, 0)),
            pl.BlockSpec((1, 1, t_, r_), lambda c: (2, jnp.clip(c * TILE - 1, 0, s_ - 1), 0, 0)),
            pl.BlockSpec((1, 1, t_, r_), lambda c: (2, jnp.minimum(c * TILE + TILE, s_ - 1), 0, 0)),
        ],
        out_specs=[
            pl.BlockSpec((wide, TILE, r_), lambda c: (0, c, 0)),
            pl.BlockSpec((ORDER + 1, wide, r_), lambda c: (0, 0, 0)),
            pl.BlockSpec((ORDER + 1, wide, r_), lambda c: (0, 0, 0)),
        ],
        out_shape=[
            jax.ShapeDtypeStruct((wide, s_ + TILE, r_), jnp.float32),
            jax.ShapeDtypeStruct((ORDER + 1, wide, r_), jnp.float32),
            jax.ShapeDtypeStruct((ORDER + 1, wide, r_), jnp.float32),
        ],
        scratch_shapes=[pltpu.VMEM((TILE * wide, r_), jnp.float32)],
        compiler_params=pltpu.CompilerParams(vmem_limit_bytes=40 << 20),
        name="source",
    )(table, velocity, velocity, velocity)


def bins_call(wall_history, phase_bin, station_of, basis, stations):
    h, s_, t_ = wall_history.shape
    step = max(d for d in range(1, 18) if h % d == 0)
    pair = 2
    def kernel(bins, x, station, base, out, acc):
        c = pl.program_id(0)

        @pl.when(c == 0)
        def _():
            acc[...] = jnp.zeros_like(acc)

        for i in range(step):
            b = bins[c * step + i]
            acc[b] += x[i]

        @pl.when(c == h // step - 1)
        def _():
            high, low = split(base[...])
            stack = jnp.concatenate([high, high, low], 0)
            pick = (lax.broadcasted_iota(jnp.int32, (stations, s_), 0) == station[...]).astype(jnp.bfloat16)

            def body(j, _):
                held = jnp.concatenate([acc[j * pair + q] for q in range(pair)], axis=1)
                top, rest = split(held)
                rows = jnp.dot(pick, top, preferred_element_type=jnp.float32) + jnp.dot(
                    pick, rest, preferred_element_type=jnp.float32
                )
                both = jnp.concatenate([rows[:, q * t_ : (q + 1) * t_] for q in range(pair)], axis=0)
                top, rest = split(both)
                tile = jnp.dot(
                    jnp.concatenate([top, rest, top], axis=1), stack, preferred_element_type=jnp.float32
                )
                for q in range(pair):
                    out[pl.ds(j * pair + q, stations, stride=NBIN), :] = tile[q * stations : (q + 1) * stations]
                return 0

            lax.fori_loop(0, NBIN // pair, body, 0, unroll=4)

    tiles = pl.pallas_call(
        kernel,
        grid_spec=pltpu.PrefetchScalarGridSpec(
            num_scalar_prefetch=1,
            grid=(h // step,),
            in_specs=[
                pl.BlockSpec((step, s_, t_), lambda c, bins: (c, 0, 0)),
                pl.BlockSpec((1, s_), lambda c, bins: (0, 0)),
                pl.BlockSpec((t_, NA), lambda c, bins: (0, 0)),
            ],
            out_specs=pl.BlockSpec((stations * NBIN, NA), lambda c, bins: (0, 0)),
            scratch_shapes=[pltpu.VMEM((NBIN, s_, t_), jnp.float32)],
        ),
        out_shape=jax.ShapeDtypeStruct((stations * NBIN, NA), jnp.float32),
        compiler_params=pltpu.CompilerParams(vmem_limit_bytes=40 << 20),
        name="bins",
    )(phase_bin, wall_history, station_of[None, :], basis)
    return tiles.reshape(stations, NBIN, NA)


def project_call(s_ext, pack_l, pack_r, velocity):
    _, s_, t_, r_ = velocity.shape
    wide = t_ + 2 * TILE
    rows = span_rows(s_)
    held = rows + (-rows) % (2 * TILE)
    out_rows = s_ + TILE
    steps = wide // TILE
    lag = TILE + ITERS
    table = np.pad(solve_table(s_), ((0, 0), (0, held - rows)))
    top = table.astype(jnp.bfloat16)
    rest = (table - top.astype(np.float32)).astype(jnp.bfloat16)
    table = jnp.asarray(np.concatenate([top, rest], 0))
    slots = TILE + 2

    def kernel(s_in, near, far, v, tab, corrected, pressure, a0, a1, a2, a3, w1, w2, w3, high, low, pot, pn, gn):
        k = pl.program_id(0)
        levels_a = [a0, a1, a2, a3]
        levels_w = [a0, w1, w2, w3]
        row = lax.broadcasted_iota(jnp.int32, (TILE, r_), 0)

        @pl.when(k == 0)
        def _():
            for ref in (a0, a1, a2, a3, w1, w2, w3):
                ref[TILE:slots] = jnp.zeros((2, rows, r_), jnp.float32)
            pot[TILE:] = jnp.zeros((TILE, out_rows, r_), jnp.float32)

        for ref in (a0, a1, a2, a3, w1, w2, w3):
            ref[0:2] = ref[TILE:slots]
        pot[:TILE] = pot[TILE:]

        def load(i, _):
            t = k * TILE + i
            own = s_in[i]
            edge = own[s_:]
            low_tile = near[pl.ds(t, TILE, stride=wide), :]
            high_tile = far[pl.ds(t, TILE, stride=wide), :]
            a0[i + 2, 0:TILE] = jnp.where(row >= TILE - ORDER, low_tile, 0.0) + jnp.where(row == TILE - 1, edge, 0.0)
            a0[i + 2, TILE : TILE + s_] = own[:s_]
            a0[i + 2, TILE : 2 * TILE] += jnp.where(row == 0, low_tile, 0.0)
            a0[i + 2, s_ : s_ + TILE] += jnp.where(row == TILE - 1, high_tile, 0.0)
            a0[i + 2, s_ + TILE : s_ + 2 * TILE] = jnp.where(row < ORDER, high_tile, 0.0) + jnp.where(row == 0, edge, 0.0)
            a0[i + 2, s_ + 2 * TILE :] = jnp.zeros((TILE, r_), jnp.float32)
            return 0

        lax.fori_loop(0, TILE, load, 0)

        for n in range(1, ITERS + 1):
            past, weighted = levels_a[n - 1], levels_w[n - 1]

            def sweep(i, _, n=n, past=past, weighted=weighted):
                total = past[i] + past[i + 2] + lane_pair(past[i + 1], 1)
                mid = weighted[i + 1]
                value = 6.0 * mid - (pltpu.roll(mid, 1, 0) + pltpu.roll(mid, rows - 1, 0)) + total
                if n < ITERS:
                    levels_a[n][i + 2] = total
                    levels_w[n][i + 2] = value
                else:
                    value = jnp.concatenate([value, jnp.zeros((held - rows, r_), jnp.float32)], 0)
                    top_part, rest_part = split(value)
                    at = pl.multiple_of(i * r_, r_)
                    high[:, pl.ds(at, r_)] = top_part
                    low[:, pl.ds(at, r_)] = rest_part
                return 0

            lax.fori_loop(0, TILE, sweep, 0)

        one = jnp.dot(tab[...], high[...], preferred_element_type=jnp.float32)
        two = jnp.dot(tab[:out_rows], low[...], preferred_element_type=jnp.float32)
        total = one[:out_rows] + one[out_rows:] + two
        for i in range(TILE):
            pot[TILE + i] = total[:, i * r_ : (i + 1) * r_]

        @pl.when(k >= 2)
        def _():
            for i in range(TILE):
                at = ITERS + i
                pn[pl.ds(i, out_rows, stride=TILE), :] = pot[at]
                gn[pl.ds(i, out_rows, stride=TILE), :] = pot[at + 1] - pot[at - 1]

            def finish(z, _):
                mid = pn[pl.ds(pl.multiple_of((z + 1) * TILE, TILE), TILE), :]
                down = pn[pl.ds(pl.multiple_of(z * TILE, TILE), TILE), :]
                up = pn[pl.ds(pl.multiple_of((z + 2) * TILE, TILE), TILE), :]
                turn = gn[pl.ds(pl.multiple_of((z + 1) * TILE, TILE), TILE), :]
                pressure[z] = mid
                corrected[0, z] = v[0, z] + 0.5 * lane_pair(mid, -1)
                corrected[1, z] = v[1, z] - 0.5 * turn
                corrected[2, z] = v[2, z] - 0.5 * (up - down)
                return 0

            lax.fori_loop(0, s_, finish, 0, unroll=8)

    at = lambda k: jnp.maximum(k - 2, 0)
    slab = pltpu.VMEM((slots, rows, r_), jnp.float32)
    return pl.pallas_call(
        kernel,
        grid=(steps,),
        in_specs=[
            pl.BlockSpec((TILE, s_ + TILE, r_), lambda k: (k, 0, 0)),
            pl.BlockSpec((TILE * wide, r_), lambda k: (0, 0)),
            pl.BlockSpec((TILE * wide, r_), lambda k: (0, 0)),
            pl.BlockSpec((3, s_, TILE, r_), lambda k: (0, 0, at(k), 0)),
            pl.BlockSpec((2 * out_rows, held), lambda k: (0, 0)),
        ],
        out_specs=[
            pl.BlockSpec((3, s_, TILE, r_), lambda k: (0, 0, at(k), 0)),
            pl.BlockSpec((s_, TILE, r_), lambda k: (0, at(k), 0)),
        ],
        out_shape=[
            jax.ShapeDtypeStruct(velocity.shape, jnp.float32),
            jax.ShapeDtypeStruct(velocity.shape[1:], jnp.float32),
        ],
        scratch_shapes=[slab] * 7
        + [
            pltpu.VMEM((held, TILE * r_), jnp.bfloat16),
            pltpu.VMEM((held, TILE * r_), jnp.bfloat16),
            pltpu.VMEM((2 * TILE, out_rows, r_), jnp.float32),
            pltpu.VMEM((out_rows * TILE, r_), jnp.float32),
            pltpu.VMEM((out_rows * TILE, r_), jnp.float32),
        ],
        compiler_params=pltpu.CompilerParams(vmem_limit_bytes=56 << 20),
        name="project",
    )(s_ext, pack_l.reshape(TILE * wide, r_), pack_r.reshape(TILE * wide, r_), velocity, table)


def azimuth_basis(first_cell, cells, total):
    column = jnp.arange(NA)
    upper = column >= NA // 2
    harmonic = jnp.where(upper, column - NA // 2 + 1, column)
    index = first_cell + jnp.arange(cells)
    phase = index[:, None] * harmonic[None, :] % total
    angle = 2.0 * math.pi / total * phase.astype(jnp.float32)
    return jnp.where(upper[None, :], jnp.sin(angle), jnp.cos(angle))


def bin_weights(scale):
    column = jnp.arange(NF)
    upper = column >= NF // 2
    harmonic = jnp.where(upper, column - NF // 2 + 1, column)
    phase = jnp.arange(NBIN)[:, None] * harmonic[None, :] % NBIN
    angle = 2.0 * math.pi / NBIN * phase.astype(jnp.float32)
    return jnp.where(upper[None, :], jnp.sin(angle), jnp.cos(angle)) * scale


def send(x, spans, planes, by_span, by_plane):
    pairs = []
    for i in range(spans):
        for j in range(planes):
            to = ((i + by_span) % spans) * planes + (j + by_plane) % planes
            pairs.append((i * planes + j, to))
    return lax.ppermute(x, ("span", "plane"), pairs)


def exchange(s_ext, zr, zl, spans, planes, span_cells, theta_cells):
    edge = ORDER + 1
    first = TILE - 1
    last = TILE + theta_cells - ORDER
    after = TILE - ORDER
    before = TILE + theta_cells - 1

    def widen(low, mid, high):
        total = mid.shape[1]
        low = jnp.pad(low, ((0, 0), (after, total - after - edge), (0, 0)))
        high = jnp.pad(high, ((0, 0), (before, total - before - edge), (0, 0)))
        return mid + low + high

    def planes_of(z, step):
        mid = send(z, spans, planes, step, 0)
        low = send(z[:, last : last + edge], spans, planes, step, 1)
        high = send(z[:, first : first + edge], spans, planes, step, -1)
        return widen(low, mid, high)

    low = send(s_ext[last : last + edge], spans, planes, 0, 1)
    high = send(s_ext[first : first + edge], spans, planes, 0, -1)
    from_left = planes_of(zr, 1)
    from_right = planes_of(zl, -1)
    hop = 1
    while hop < spans and np.any(hop_table(hop * span_cells)):
        table = hop_table(hop * span_cells)
        far_left = planes_of(zr, hop + 1)
        far_right = planes_of(zl, -hop - 1)
        from_left = from_left.at[1:].add(
            jnp.einsum("bd,dar->bar", table[::-1], jnp.concatenate([far_left[:1], far_left[:0:-1]], 0), precision=PRECISE))
        from_right = from_right.at[:-1].add(
            jnp.einsum("bd,dar->bar", table, jnp.concatenate([far_right[-1:], far_right[:-1]], 0), precision=PRECISE))
        hop += 1
    s_ext = s_ext.at[after : after + edge].add(low).at[before : before + edge].add(high)
    gap = jnp.zeros((2,) + zr.shape[1:], zr.dtype)
    pack_l = jnp.concatenate([from_left[:1], gap, from_left[1:]], 0)
    pack_r = jnp.concatenate([from_right[:-1], gap, from_right[-1:]], 0)
    return s_ext, pack_l, pack_r


def local(velocity, wall_history, phase_bin, station_of, wall_index, spans, planes):
    _, span_cells, theta_cells, _ = velocity.shape
    total_theta = theta_cells * planes
    stations = ST_DEV * spans
    basis = azimuth_basis(lax.axis_index("plane") * theta_cells, theta_cells, total_theta)
    s_ext, zr, zl = source_call(velocity)
    tiles = bins_call(wall_history, phase_bin, station_of, basis, stations)
    s_ext, pack_l, pack_r = exchange(s_ext, zr, zl, spans, planes, span_cells, theta_cells)
    held = lax.psum_scatter(tiles, "span", scatter_dimension=0, tiled=True)
    held = lax.psum(held, "plane")
    corrected, pressure = project_call(s_ext, pack_l, pack_r, velocity)
    wall_select = (wall_index[:, None] == jnp.arange(WALL_SPAN)[None, :]).astype(jnp.float32)
    wall = jnp.sum(pressure[:, :, :WALL_SPAN] * wall_select[None, :, :], axis=2)
    selector = (station_of[:, None] == jnp.arange(stations)[None, :]).astype(jnp.float32)
    wall_tile = jnp.dot(jnp.dot(selector.T, wall, precision=PRECISE), basis, precision=PRECISE)
    wall_tile = lax.psum(lax.psum_scatter(wall_tile, "span", scatter_dimension=0, tiled=True), "plane")
    newest = (jnp.arange(NBIN) == phase_bin[-1]).astype(jnp.float32)
    held = held + newest[None, :, None] * wall_tile[:, None, :]
    weights = bin_weights(1.0 / math.sqrt(total_theta * (wall_history.shape[0] + 1)))
    coefficients = jnp.einsum("sba,bf->saf", held, weights, precision=PRECISE).reshape(ST_DEV, NA * NF)
    return corrected, pressure, coefficients


def solution(mesh):
    spans = mesh.shape["span"]
    planes = mesh.shape["plane"]
    in_specs = (
        P(None, "span", "plane", None),
        P(None, "span", "plane"),
        P(),
        P("span"),
        P("plane"),
    )
    out_specs = (P(None, "span", "plane", None), P("span", "plane", None), P("span", None))

    def body(*args):
        return local(*args, spans, planes)

    return jax.shard_map(body, mesh=mesh, in_specs=in_specs, out_specs=out_specs, check_vma=False)
```

time: 1280 us -> 264 us (0.21)
  waiting for transfers between devices: 401 us -> 27.4 us
  blocking collectives: 379 us -> 40.8 us
  local copies, waits for them, and re-layouts: 189 us -> 2.8 us
  Pallas kernels: 0 us -> 150 us
  matrix products: 137 us -> 2.39 us
  other arithmetic: 117 us -> 11.7 us
  starting transfers between devices: 30 us -> 13.3 us
    all_to_all x2 -> x0, blocking collectives: 379 us -> none  [the longest x1 190 us: local(): lax.all_to_all(source, 'span', split_axis=1, concat_axis=0, tiled=True)]
    all_to_all x2 -> x0, waiting for transfers between devices: 348 us -> none  [the longest x1 184 us: local(): lax.all_to_all(spectra_lines, 'span', split_axis=0, concat_axis=1, tiled=...]
    pallas_call x0 -> x3, Pallas kernels: none -> 150 us  [the longest x1 106 us: project_call(): pl.pallas_call(kernel, grid=(steps,), in_specs=[pl.BlockSpec((TILE, s_ +...]
    dot_general x5 -> x3, matrix products: 137 us -> 2.39 us  [the longest x1 1.62 us: local(): jnp.einsum('sba,bf->saf', held, weights, precision=PRECISE)]
    unnamed x23 -> x14, local copies, waits for them, and re-layouts: 104 us -> 1.3 us
    div x5 -> x0, other arithmetic: 49.1 us -> none  [the longest x4 47.7 us: local(): (spectra + padded[:, :-2, :] + padded[:, 2:, :] + radial_pair(potential))...]
    unnamed x3 -> x2, waiting for transfers between devices: 46 us -> 0.03 us
    unnamed x0 -> x1, blocking collectives: none -> 35.1 us
  transfers between devices with their start and end apart: 20 -> 10, of which waited for: 7 -> 3; matrix products, arithmetic and copies ran while one was open for 16% -> 5% of each run, Pallas kernels for 0% -> 47%
where the time goes in v1:
time: 264 us; the launch traced here: 263 us
  Pallas kernels  150 us (57%)
  blocking collectives  40.8 us (15%)
  waiting for transfers between devices  27.4 us (10%)
  between operations  14.9 us (6%)
  starting transfers between devices  13.3 us (5%)
  other arithmetic  11.7 us (4%)
  local copies, waits for them, and re-layouts  2.8 us (1%)
    pallas_call x1, Pallas kernels, project_call(): pl.pallas_call(kernel, grid=(steps,), in_specs=[pl.BlockSpec((TILE, s_ +...  106 us
    unnamed x1, blocking collectives  35.1 us
    pallas_call x1, Pallas kernels, source_call(): pl.pallas_call(kernel, grid=(blocks + 1,), in_specs=[pl.BlockSpec(memory_...  27.5 us
    psum x1, waiting for transfers between devices, local(): held = lax.psum(held, 'plane')  23.1 us
    pallas_call x1, Pallas kernels, bins_call(): pl.pallas_call(kernel, grid_spec=pltpu.PrefetchScalarGridSpec(num_scalar_...  16.9 us
    ppermute x8, starting transfers between devices, send(): return lax.ppermute(x, ('span', 'plane'), pairs)  13.2 us
    psum x1, blocking collectives, local(): lax.psum(lax.psum_scatter(wall_tile, 'span', scatter_dimension=0, tiled=T...  5.67 us
    reduce_sum x1, other arithmetic, local(): wall = jnp.sum(pressure[:, :, :WALL_SPAN] * wall_select[None, :, :], axis=2)  5.63 us
  transfers between devices with their start and end apart: 10, of which 3 were waited for; matrix products, arithmetic and copies ran while one was open for 5% of the time, Pallas kernels for 47%

profile of v1, /device:TPU:0, one launch (start us, length us, event | category | flops | bytes accessed | tf_op | source)
XLA Modules:
  0.0 263.5 jit_solution(17455416657533867545)
XLA Ops:
  7.2 0.0 reduce-scatter.2.cloned.1.call-start
  7.2 0.0 copy-start.1
  7.2 0.7 copy-done.1
  7.9 0.0 copy-start.2
  7.9 0.0 copy-start.3
  7.9 27.5 %source.1 = (f32[144,136,128]{2,1,0:T(8,128)S(1)}, f32[6,144,128]{2,1,0:T(8,128)S(1)}, f32[6,144,128]{2,1,0:T(8,128)S(1)}) custom-call(f32[5,128]{1,0:T(8,128)S(1)} %copy-done.1, f32[3,128,128,128]{3,2,1,0:T(8,128)} %v.3, f32[3,128,128,128]{3,2,1,0:T(8,128)} %v.3, f32[3,128,128,128]{3,2,1,0:T(8,128)} %v.3), custom_call_target="tpu_custom_call" | custom-call | tf_op jit(solution)/shard_map/source/pallas_call | solution.py:160
  35.4 0.0 copy-start
  35.4 0.0 copy-start.4
  35.4 0.0 copy-start.5
  35.4 3.0 %collective-permute-start.2 = (f32[6,144,128]{2,1,0:T(8,128)S(1)}, f32[6,144,128]{2,1,0:T(8,128)S(1)}, u32[]{:S(2)}, u32[]{:S(2)}) collective-permute-start(f32[6,144,128]{2,1,0:T(8,128)S(1)} %get-tuple-element.33), channel_id=1, source_target_pairs={{0,4},{1,5},{2,6},{3,7},{4,8},{5,9},{6,10},{7,11},{8,12},{9,13},{1... | collective-permute-start | bytes 1327112 | tf_op jit(solution)/shard_map/ppermute | solution.py:393
  38.4 0.8 collective-permute-start.3
  39.2 3.0 %collective-permute-start.4 = (f32[6,6,128]{2,1,0:T(8,128)S(1)}, f32[6,6,128]{2,1,0:T(8,128)S(1)}, u32[]{:S(2)}, u32[]{:S(2)}) collective-permute-start(f32[6,6,128]{2,1,0:T(8,128)S(1)} %get-tuple-element.42), channel_id=1, source_target_pairs={{0,7},{1,4},{2,5},{3,6},{4,11},{5,8},{6,9},{7,10},{8,15},{9,12},{1... | collective-permute-start | bytes 55304 | tf_op jit(solution)/shard_map/ppermute | solution.py:393
  42.1 3.2 %collective-permute-start.5 = (f32[6,144,128]{2,1,0:T(8,128)S(1)}, f32[6,144,128]{2,1,0:T(8,128)S(1)}, u32[]{:S(2)}, u32[]{:S(2)}) collective-permute-start(f32[6,144,128]{2,1,0:T(8,128)S(1)} %get-tuple-element.34), channel_id=1, source_target_pairs={{0,28},{1,29},{2,30},{3,31},{4,0},{5,1},{6,2},{7,3},{8,4},{9,5},{1... | collective-permute-start | bytes 1327112 | tf_op jit(solution)/shard_map/ppermute | solution.py:393
  45.4 0.0 copy-done
  45.4 0.1 collective-permute-start
  45.5 0.3 cosine_select_fusion.base
  45.8 0.0 copy-done.2
  45.9 0.0 copy-done.3
  45.9 16.9 %bins.2 = f32[2048,128]{1,0:T(8,128)} custom-call(s32[256]{0:T(256)S(1)} %copy-done.3, f32[255,128,128]{2,1,0:T(8,128)} %x.9, s32[1,128]{1,0:T(1,128)S(1)} %bitcast.11, f32[128,128]{1,0:T(8,128)S(1)} %cosine_select_fusion.base), custom_call_target="tpu_custom_call" | custom-call | tf_op jit(solution)/shard_map/bins/pallas_call | solution.py:223
  62.7 0.0 reduce-scatter.2.cloned.1.call-update
  62.7 0.0 all-reduce.7.cloned.1.call-start
  62.8 0.6 slice.96
  63.4 0.0 copy-done.4
  63.4 0.1 fusion.10
  63.5 0.7 compare_convert_fusion
  64.2 0.0 copy-done.5
  64.2 0.6 dynamic-slice.16
  65.4 0.0 collective-permute-done
  65.4 1.7 collective-permute-start.6
  67.2 2.0 fusion.43
  69.2 0.0 collective-permute-done.3
  69.2 0.8 collective-permute-start.7
  69.9 0.0 collective-permute-done.4
  69.9 0.7 collective-permute-start.1
  70.6 0.0 collective-permute-done.2
  70.7 0.0 collective-permute-done.6
  70.7 1.8 collective-permute-done.7
  72.6 0.0 collective-permute-done.5
  72.7 1.1 pad_maximum_fusion.1
  73.8 2.4 collective-permute-done.1
  76.2 1.8 fusion.s_in
  78.0 105.9 %project.1 = (f32[3,128,128,128]{3,2,1,0:T(8,128)}, f32[128,128,128]{2,1,0:T(8,128)}) custom-call(f32[144,136,128]{2,1,0:T(8,128)} %fusion.s_in, f32[1152,128]{1,0:T(8,128)} %bitcast.13, f32[1152,128]{1,0:T(8,128)} %bitcast.12, f32[3,128,128,128]{3,2,1,0:T(8,128)} %v.3, bf16[272,160]{1,0:T(8,128)(2,1)} %constant.118.clone.tab), custom_call_target="tpu_custom_call" | custom-call | tf_op jit(solution)/shard_map/project/pallas_call | solution.py:337
  183.8 5.6 %multiply_reduce_fusion = f32[128,128]{1,0:T(8,128)S(1)} fusion(f32[128,128,128]{2,1,0:T(8,128)} %get-tuple-element.30, f32[128,8]{1,0:T(8,128)S(1)} %fusion.10), kind=kLoop, calls=%fused_computation | loop fusion | flops 245760 | bytes 593920 | tf_op jit(solution)/shard_map/reduce_sum | solution.py:448
  189.5 0.3 fusion.9
  189.8 0.5 fusion.26
  190.3 35.1 %all-reduce.4 = f32[32,128]{1,0:T(8,128)S(1)} all-reduce(f32[32,128]{1,0:T(8,128)S(1)} %fusion.26), channel_id=3, replica_groups=mesh['span'=8,'plane'=4] {'span'}, use_global_device_ids=true, to_apply=%region_3.4.clone | all-reduce | flops 4096 | bytes 32768
  225.4 0.0 reduce-scatter.2.cloned.1.call-done
  225.4 0.0 all-reduce.7.cloned.1.call-update
  225.4 5.7 %psum.15 = f32[4,128]{1,0:T(4,128)S(1)} all-reduce(f32[4,128]{1,0:T(4,128)S(1)} %constant_dynamic-slice_fusion), channel_id=1, replica_groups=mesh['span'=8,'plane'=4] {'plane'}, use_global_device_ids=true, to_apply=%region_4.5 | all-reduce | flops 512 | bytes 4096 | tf_op jit(solution)/shard_map/psum | solution.py:451
  231.1 23.1 %all-reduce.7.cloned.1.call-done = f32[4,64,128]{2,1,0:T(8,128)} async-done(((f32[4,64,128]{2,1,0:T(8,128)}), f32[4,64,128]{2,1,0:T(8,128)}) %all-reduce.7.cloned.1.call-update) | async-done | bytes 131088 | tf_op jit(solution)/shard_map/psum | solution.py:445
  254.2 1.6 fusion.1
  255.8 0.8 reshape.132
  (14 shorter events, 0.2 us)
Async XLA Ops:
  7.2 218.2 %reduce-scatter.2.cloned.1.call-start = ((), (), s32[]{:S(2)}) async-start(), calls=%async_computation.1 | async-start | bytes 1179648 | tf_op jit(solution)/shard_map/reduce_scatter | solution.py:444
  7.2 0.7 copy-start.1
  7.9 37.9 %copy-start.2 = (s32[128]{0:T(128)S(1)}, s32[128]{0:T(128)}, u32[]{:S(2)}) copy-start(s32[128]{0:T(128)} %param.14) | copy-start | bytes 1540
  7.9 38.0 %copy-start.3 = (s32[256]{0:T(256)S(1)}, s32[256]{0:T(256)}, u32[]{:S(2)}) copy-start(s32[256]{0:T(256)} %bins.3) | copy-start | bytes 3076
  35.4 10.0 %copy-start = (f32[144,136,128]{2,1,0:T(8,128)}, f32[144,136,128]{2,1,0:T(8,128)S(1)}, u32[]{:S(2)}) copy-start(f32[144,136,128]{2,1,0:T(8,128)S(1)} %get-tuple-element.32) | copy-start | bytes 30081028
  35.4 28.0 %copy-start.4 = (s32[128]{0:T(128)S(1)}, s32[128]{0:T(128)}, u32[]{:S(2)}) copy-start(s32[128]{0:T(128)} %param.15) | copy-start | bytes 1540
  35.4 28.8 %copy-start.5 = (u32[32]{0:T(128)S(1)}, u32[32]{0:T(128)}, u32[]{:S(2)}) copy-start(u32[32]{0:T(128)} %constant.129) | copy-start | bytes 388
  35.4 35.2 %collective-permute-start.2 = (f32[6,144,128]{2,1,0:T(8,128)S(1)}, f32[6,144,128]{2,1,0:T(8,128)S(1)}, u32[]{:S(2)}, u32[]{:S(2)}) collective-permute-start(f32[6,144,128]{2,1,0:T(8,128)S(1)} %get-tuple-element.33), channel_id=1, source_target_pairs={{0,4},{1,5},{2,6},{3,7},{4,8},{5,9},{6,10},{7,11},{8,12},{9,13},{1... | collective-permute-start | bytes 1327112 | tf_op jit(solution)/shard_map/ppermute | solution.py:393
  38.4 30.7 %collective-permute-start.3 = (f32[6,6,128]{2,1,0:T(8,128)S(1)}, f32[6,6,128]{2,1,0:T(8,128)S(1)}, u32[]{:S(2)}, u32[]{:S(2)}) collective-permute-start(f32[6,6,128]{2,1,0:T(8,128)S(1)} %get-tuple-element.41), channel_id=1, source_target_pairs={{0,5},{1,6},{2,7},{3,4},{4,9},{5,10},{6,11},{7,8},{8,13},{9,14},{1... | collective-permute-start | bytes 55304 | tf_op jit(solution)/shard_map/ppermute | solution.py:393
  39.2 30.7 %collective-permute-start.4 = (f32[6,6,128]{2,1,0:T(8,128)S(1)}, f32[6,6,128]{2,1,0:T(8,128)S(1)}, u32[]{:S(2)}, u32[]{:S(2)}) collective-permute-start(f32[6,6,128]{2,1,0:T(8,128)S(1)} %get-tuple-element.42), channel_id=1, source_target_pairs={{0,7},{1,4},{2,5},{3,6},{4,11},{5,8},{6,9},{7,10},{8,15},{9,12},{1... | collective-permute-start | bytes 55304 | tf_op jit(solution)/shard_map/ppermute | solution.py:393
  42.1 30.4 %collective-permute-start.5 = (f32[6,144,128]{2,1,0:T(8,128)S(1)}, f32[6,144,128]{2,1,0:T(8,128)S(1)}, u32[]{:S(2)}, u32[]{:S(2)}) collective-permute-start(f32[6,144,128]{2,1,0:T(8,128)S(1)} %get-tuple-element.34), channel_id=1, source_target_pairs={{0,28},{1,29},{2,30},{3,31},{4,0},{5,1},{6,2},{7,3},{8,4},{9,5},{1... | collective-permute-start | bytes 1327112 | tf_op jit(solution)/shard_map/ppermute | solution.py:393
  45.4 20.0 %collective-permute-start = (f32[6,136,128]{2,1,0:T(8,128)S(1)}, f32[6,136,128]{2,1,0:T(8,128)S(1)}, u32[]{:S(2)}, u32[]{:S(2)}) collective-permute-start(f32[6,136,128]{2,1,0:T(8,128)S(1)} %slice.85), channel_id=1, source_target_pairs={{0,1},{1,2},{2,3},{3,0},{4,5},{5,6},{6,7},{7,4},{8,9},{9,10},{10,1... | collective-permute-start | bytes 1253384 | tf_op jit(solution)/shard_map/ppermute | solution.py:393
  62.7 191.5 %all-reduce.7.cloned.1.call-start = ((), (), s32[]{:S(2)}) async-start(), calls=%async_computation.2 | async-start | bytes 262144 | tf_op jit(solution)/shard_map/psum | solution.py:445
  65.4 5.3 %collective-permute-start.6 = (f32[6,6,128]{2,1,0:T(8,128)S(1)}, f32[6,6,128]{2,1,0:T(8,128)S(1)}, u32[]{:S(2)}, u32[]{:S(2)}) collective-permute-start(f32[6,6,128]{2,1,0:T(8,128)S(1)} %get-tuple-element.39), channel_id=1, source_target_pairs={{0,29},{1,30},{2,31},{3,28},{4,1},{5,2},{6,3},{7,0},{8,5},{9,6},{1... | collective-permute-start | bytes 55304 | tf_op jit(solution)/shard_map/ppermute | solution.py:393
  69.2 3.4 %collective-permute-start.7 = (f32[6,6,128]{2,1,0:T(8,128)S(1)}, f32[6,6,128]{2,1,0:T(8,128)S(1)}, u32[]{:S(2)}, u32[]{:S(2)}) collective-permute-start(f32[6,6,128]{2,1,0:T(8,128)S(1)} %get-tuple-element.40), channel_id=1, source_target_pairs={{0,31},{1,28},{2,29},{3,30},{4,3},{5,0},{6,1},{7,2},{8,7},{9,4},{1... | collective-permute-start | bytes 55304 | tf_op jit(solution)/shard_map/ppermute | solution.py:393
  69.9 6.2 %collective-permute-start.1 = (f32[6,136,128]{2,1,0:T(8,128)S(1)}, f32[6,136,128]{2,1,0:T(8,128)S(1)}, u32[]{:S(2)}, u32[]{:S(2)}) collective-permute-start(f32[6,136,128]{2,1,0:T(8,128)S(1)} %get-tuple-element.37), channel_id=1, source_target_pairs={{0,3},{1,0},{2,1},{3,2},{4,7},{5,4},{6,5},{7,6},{8,11},{9,8},{10,9... | collective-permute-start | bytes 1253384 | tf_op jit(solution)/shard_map/ppermute | solution.py:393
Sparse Core Ops, SparseCore 0:
  62.9 61.3 reduce-scatter.1
  225.5 28.6 all-reduce.6

commit v2 on v1

v2 whole, which is shorter than its diff:
```python
import math

import jax
import jax.numpy as jnp
import numpy as np
from jax import lax
from jax.experimental import pallas as pl
from jax.experimental.pallas import tpu as pltpu
from jax.sharding import PartitionSpec as P

NZ = 1024
NA = 128
NF = 64
NBIN = 64
ITERS = 4
WALL_SPAN = 8
ST_DEV = 4
ORDER = ITERS + 1
TILE = 8
LEAD = 9
RHO = 3.0 - 2.0 * math.sqrt(2.0)
PRECISE = lax.Precision.HIGHEST


def representable(table):
    table = np.asarray(table, np.float64)
    return np.where(np.abs(table) < np.finfo(np.float32).tiny, 0.0, table).astype(np.float32)


def inverse_entry(distance, order=ORDER):
    j = order - 1
    return RHO ** (order + distance) * sum(
        math.comb(j + i, j) * math.comb(j + distance + i, j) * RHO ** (2 * i) for i in range(40)
    )


def carry_weight(node, distance):
    basis = 1.0
    for other in range(ORDER):
        if other != node:
            basis *= (distance - other) / (node - other)
    return RHO ** (distance - node) * basis


def carry_table(cells):
    return representable([[carry_weight(b, d) for d in range(cells)] for b in range(ORDER)])


def hop_table(offset):
    return representable([[carry_weight(b, offset + d) for d in range(-1, ORDER)] for b in range(ORDER)])


def radial_modes(cells):
    index = np.arange(1, cells + 1)
    return math.sqrt(2.0 / (cells + 1)) * np.sin(np.pi * np.outer(index, index) / (cells + 1))


def radial_rates(cells):
    return (2.0 * np.cos(np.pi * np.arange(1, cells + 1) / (cells + 1))).astype(np.float32)


def radial_step(cells):
    return 0.5 * (np.eye(cells, k=-1) - np.eye(cells, k=1))


def stacked(table):
    table = np.asarray(table, np.float32)
    top = table.astype(jnp.bfloat16)
    rest = (table - top.astype(np.float32)).astype(jnp.bfloat16)
    return np.concatenate([top, top, rest], 0)


def span_rows(cells):
    return cells + 3 * TILE


def solve_table(cells):
    rows = span_rows(cells)
    table = np.zeros((cells + TILE, rows))
    entries = [inverse_entry(d) for d in range(cells + 2 * TILE)]
    for i in range(cells + 2):
        for z in range(-ORDER - ITERS, cells + ORDER + ITERS):
            table[i, (z + TILE) % rows] = entries[abs(i - 1 - z)]
    return representable(table)


def wall_table(cells):
    table = np.zeros((ORDER, cells, cells + 2 * TILE))
    for j in range(ORDER):
        entries = [inverse_entry(d, j + 1) for d in range(cells + ORDER)]
        for i in range(cells):
            for z in range(-ORDER, cells + ORDER):
                table[j, i, z + TILE] = entries[abs(i - z)]
    return representable(table)


def split(x):
    high = x.astype(jnp.bfloat16)
    low = (x - high.astype(jnp.float32)).astype(jnp.bfloat16)
    return high, low


def triple(x):
    high, low = split(x)
    return jnp.concatenate([high, low, high], axis=1)


def source_call(velocity):
    _, s_, t_, r_ = velocity.shape
    wide = t_ + 2 * TILE
    blocks = t_ // TILE
    tall = s_ + TILE
    modes = radial_modes(r_)
    both = jnp.asarray(np.concatenate([stacked(-radial_step(r_) @ modes), stacked(modes)], 0))
    carry = carry_table(s_)
    table = np.zeros((2 * TILE, s_), np.float32)
    for b in range(ORDER):
        table[TILE - 1 - b] = carry[b, ::-1]
        table[TILE + b] = carry[b]
    top = table.astype(jnp.bfloat16)
    rest = (table - top.astype(np.float32)).astype(jnp.bfloat16)
    table = jnp.asarray(np.concatenate([top, rest], 0))

    def kernel(radial, turn, along, tab, both_ref, s_out, zr, zl, keep, hold, lhs, high, low):
        k = pl.program_id(0)

        @pl.when(k == 0)
        def _():
            keep[...] = jnp.zeros_like(keep)
            hold[...] = jnp.zeros_like(hold)
            s_out[...] = jnp.zeros_like(s_out)
            zr[...] = jnp.zeros_like(zr)
            zl[...] = jnp.zeros_like(zl)

        @pl.when(k > 0)
        def _():
            inside = k <= blocks
            pad = jnp.zeros((TILE, r_), jnp.float32)
            for i in range(TILE):
                at = pl.ds(i, s_, stride=TILE)
                x0, x1, x2 = radial[at, :], turn[at, :], along[at, :]
                x0 = jnp.where(inside, x0, 0.0)
                x1 = jnp.where(inside, x1, 0.0)
                x2 = jnp.concatenate([jnp.where(inside, x2, 0.0), pad], 0)
                across = jnp.concatenate([0.5 * (keep[0] - x1), pad], 0)
                lhs[i * tall : (i + 1) * tall, 3 * r_ :] = triple(hold[...] + across)
                hold[...] = 0.5 * (pltpu.roll(x2, 1, 0) - pltpu.roll(x2, tall - 1, 0))
                keep[0] = keep[1]
                keep[1] = x1
                lhs[i * tall : (i + 1) * tall, : 3 * r_] = triple(jnp.concatenate([keep[2], pad], 0))
                keep[2] = x0
            value = jnp.dot(lhs[...], both_ref[...], preferred_element_type=jnp.float32)
            for i in range(TILE):
                own = value[i * tall : (i + 1) * tall]
                s_out[i] = own
                top, rest = split(own[:s_])
                high[:, i * r_ : (i + 1) * r_] = top
                low[:, i * r_ : (i + 1) * r_] = rest
            one = jnp.dot(tab[...], high[...], preferred_element_type=jnp.float32)
            two = jnp.dot(tab[: 2 * TILE], low[...], preferred_element_type=jnp.float32)
            planes = one[: 2 * TILE] + one[2 * TILE :] + two
            row = lax.broadcasted_iota(jnp.int32, (TILE, r_), 0)
            for i in range(TILE):
                edge = s_out[i, s_:]
                here = planes[:, i * r_ : (i + 1) * r_]
                zr[i] = here[:TILE] + jnp.where(row == 0, edge, 0.0)
                zl[i] = here[TILE:] + jnp.where(row == TILE - 1, edge, 0.0)

    def part(axis):
        return pl.BlockSpec((1, s_, TILE, r_), lambda k: (axis, 0, jnp.clip(k - 1, 0, blocks - 1), 0))

    def flat(ref):
        return ref.reshape(s_ * TILE, r_)

    def body(x0, x1, x2, *refs):
        kernel(flat(x0.at[0]), flat(x1.at[0]), flat(x2.at[0]), *refs)

    return pl.pallas_call(
        body,
        grid=(wide // TILE,),
        in_specs=[
            part(0),
            part(1),
            part(2),
            pl.BlockSpec((4 * TILE, s_), lambda k: (0, 0)),
            pl.BlockSpec((6 * r_, r_), lambda k: (0, 0)),
        ],
        out_specs=[
            pl.BlockSpec((TILE, tall, r_), lambda k: (k, 0, 0)),
            pl.BlockSpec((TILE, TILE, r_), lambda k: (k, 0, 0)),
            pl.BlockSpec((TILE, TILE, r_), lambda k: (k, 0, 0)),
        ],
        out_shape=[
            jax.ShapeDtypeStruct((wide, tall, r_), jnp.float32),
            jax.ShapeDtypeStruct((wide, TILE, r_), jnp.float32),
            jax.ShapeDtypeStruct((wide, TILE, r_), jnp.float32),
        ],
        scratch_shapes=[
            pltpu.VMEM((3, s_, r_), jnp.float32),
            pltpu.VMEM((tall, r_), jnp.float32),
            pltpu.VMEM((TILE * tall, 6 * r_), jnp.bfloat16),
            pltpu.VMEM((s_, TILE * r_), jnp.bfloat16),
            pltpu.VMEM((s_, TILE * r_), jnp.bfloat16),
        ],
        compiler_params=pltpu.CompilerParams(vmem_limit_bytes=40 << 20),
        name="source",
    )(velocity, velocity, velocity, table, both)


def bins_call(wall_history, phase_bin, station_of, basis, stations):
    h, s_, t_ = wall_history.shape
    step = max(d for d in range(1, 52) if h % d == 0)
    pair = 2
    def kernel(bins, x, station, base, out, acc):
        c = pl.program_id(0)

        @pl.when(c == 0)
        def _():
            acc[...] = jnp.zeros_like(acc)

        for i in range(step):
            b = bins[c * step + i]
            acc[b] += x[i]

        @pl.when(c == h // step - 1)
        def _():
            high, low = split(base[...])
            stack = jnp.concatenate([high, high, low], 0)
            pick = (lax.broadcasted_iota(jnp.int32, (stations, s_), 0) == station[...]).astype(jnp.bfloat16)

            def body(j, _):
                held = jnp.concatenate([acc[j * pair + q] for q in range(pair)], axis=1)
                top, rest = split(held)
                rows = jnp.dot(pick, top, preferred_element_type=jnp.float32) + jnp.dot(
                    pick, rest, preferred_element_type=jnp.float32
                )
                both = jnp.concatenate([rows[:, q * t_ : (q + 1) * t_] for q in range(pair)], axis=0)
                top, rest = split(both)
                tile = jnp.dot(
                    jnp.concatenate([top, rest, top], axis=1), stack, preferred_element_type=jnp.float32
                )
                for q in range(pair):
                    out[pl.ds(j * pair + q, stations, stride=NBIN), :] = tile[q * stations : (q + 1) * stations]
                return 0

            lax.fori_loop(0, NBIN // pair, body, 0, unroll=4)

    tiles = pl.pallas_call(
        kernel,
        grid_spec=pltpu.PrefetchScalarGridSpec(
            num_scalar_prefetch=1,
            grid=(h // step,),
            in_specs=[
                pl.BlockSpec((step, s_, t_), lambda c, bins: (c, 0, 0)),
                pl.BlockSpec((1, s_), lambda c, bins: (0, 0)),
                pl.BlockSpec((t_, NA), lambda c, bins: (0, 0)),
            ],
            out_specs=pl.BlockSpec((stations * NBIN, NA), lambda c, bins: (0, 0)),
            scratch_shapes=[pltpu.VMEM((NBIN, s_, t_), jnp.float32)],
        ),
        out_shape=jax.ShapeDtypeStruct((stations * NBIN, NA), jnp.float32),
        compiler_params=pltpu.CompilerParams(vmem_limit_bytes=40 << 20),
        name="bins",
    )(phase_bin, wall_history, station_of[None, :], basis)
    return tiles.reshape(stations, NBIN, NA)


def slab_parts(own, low, high, cells):
    row = lax.broadcasted_iota(jnp.int32, (TILE, own.shape[-1]), 0)
    edge = own[cells:]
    before = jnp.where(row >= TILE - ORDER, low, 0.0) + jnp.where(row == TILE - 1, edge, 0.0)
    after = jnp.where(row < ORDER, high, 0.0) + jnp.where(row == 0, edge, 0.0)
    return before, jnp.where(row == 0, low, 0.0), jnp.where(row == TILE - 1, high, 0.0), after


def project_call(s_ext, pack_l, pack_r, velocity):
    _, s_, t_, r_ = velocity.shape
    wide = t_ + 2 * TILE
    rows = span_rows(s_)
    held = rows + (-rows) % (2 * TILE)
    out_rows = s_ + TILE
    steps = wide // TILE
    table = np.pad(solve_table(s_), ((0, 0), (0, held - rows)))
    top = table.astype(jnp.bfloat16)
    rest = (table - top.astype(np.float32)).astype(jnp.bfloat16)
    table = jnp.asarray(np.concatenate([top, rest], 0))
    modes = radial_modes(r_)
    back = jnp.asarray(np.concatenate([stacked(modes), stacked(modes @ radial_step(r_))], 1))
    rates = jnp.asarray(radial_rates(r_))[None, :]
    slots = TILE + 2

    def kernel(s_in, near, far, v, tab, turn, rate, corrected, pressure, *scratch):
        a0, a1, a2, a3, w1, w2, w3, high, low, pot, rad, pn, gn, rn = scratch
        k = pl.program_id(0)
        levels_a = [a0, a1, a2, a3]
        levels_w = [a0, w1, w2, w3]

        @pl.when(k == 0)
        def _():
            for ref in (a0, a1, a2, a3, w1, w2, w3):
                ref[TILE:slots] = jnp.zeros((2, rows, r_), jnp.float32)
            a0[:, rows - TILE :] = jnp.zeros((slots, TILE, r_), jnp.float32)
            pot[TILE:] = jnp.zeros((TILE, out_rows, r_), jnp.float32)
            rad[TILE:] = jnp.zeros((TILE, out_rows, r_), jnp.float32)

        for ref in (a0, a1, a2, a3, w1, w2, w3):
            ref[0:2] = ref[TILE:slots]
        pot[:TILE] = pot[TILE:]
        rad[:TILE] = rad[TILE:]

        def load(i, _):
            own = s_in[i]
            before, at_low, at_high, after = slab_parts(own, near[i], far[i], s_)
            a0[i + 2, 0:TILE] = before
            a0[i + 2, TILE : TILE + s_] = own[:s_]
            a0[i + 2, TILE : 2 * TILE] += at_low
            a0[i + 2, s_ : s_ + TILE] += at_high
            a0[i + 2, s_ + TILE : s_ + 2 * TILE] = after
            return 0

        lax.fori_loop(0, TILE, load, 0)

        for n in range(1, ITERS + 1):
            past, weighted = levels_a[n - 1], levels_w[n - 1]

            def sweep(i, _, n=n, past=past, weighted=weighted):
                total = past[i] + past[i + 2] + rate[...] * past[i + 1]
                mid = weighted[i + 1]
                value = 6.0 * mid - (pltpu.roll(mid, 1, 0) + pltpu.roll(mid, rows - 1, 0)) + total
                if n < ITERS:
                    levels_a[n][i + 2] = total
                    levels_w[n][i + 2] = value
                else:
                    value = jnp.concatenate([value, jnp.zeros((held - rows, r_), jnp.float32)], 0)
                    top_part, rest_part = split(value)
                    at = pl.multiple_of(i * r_, r_)
                    high[:, pl.ds(at, r_)] = top_part
                    low[:, pl.ds(at, r_)] = rest_part
                return 0

            lax.fori_loop(0, TILE, sweep, 0)

        one = jnp.dot(tab[...], high[...], preferred_element_type=jnp.float32)
        two = jnp.dot(tab[:out_rows], low[...], preferred_element_type=jnp.float32)
        total = one[:out_rows] + one[out_rows:] + two
        for i in range(TILE):
            here = jnp.dot(triple(total[:, i * r_ : (i + 1) * r_]), turn[...], preferred_element_type=jnp.float32)
            pot[TILE + i] = here[:, :r_]
            rad[TILE + i] = here[:, r_:]

        @pl.when(k >= 2)
        def _():
            for i in range(TILE):
                at = LEAD - ORDER + 1 + i
                pn[pl.ds(i, out_rows, stride=TILE), :] = pot[at]
                rn[pl.ds(i, out_rows, stride=TILE), :] = rad[at]
                gn[pl.ds(i, out_rows, stride=TILE), :] = 0.5 * (pot[at + 1] - pot[at - 1])

            def finish(z, _):
                here = pl.ds(pl.multiple_of((z + 1) * TILE, TILE), TILE)
                down = pn[pl.ds(pl.multiple_of(z * TILE, TILE), TILE), :]
                up = pn[pl.ds(pl.multiple_of((z + 2) * TILE, TILE), TILE), :]
                pressure[z] = pn[here, :]
                corrected[0, z] = v[0, z] - rn[here, :]
                corrected[1, z] = v[1, z] - gn[here, :]
                corrected[2, z] = v[2, z] - 0.5 * (up - down)
                return 0

            lax.fori_loop(0, s_, finish, 0, unroll=8)

    at = lambda k: jnp.maximum(k - 2, 0)
    slab = pltpu.VMEM((slots, rows, r_), jnp.float32)
    return pl.pallas_call(
        kernel,
        grid=(steps,),
        in_specs=[
            pl.BlockSpec((TILE, s_ + TILE, r_), lambda k: (k, 0, 0)),
            pl.BlockSpec((TILE, TILE, r_), lambda k: (k, 0, 0)),
            pl.BlockSpec((TILE, TILE, r_), lambda k: (k, 0, 0)),
            pl.BlockSpec((3, s_, TILE, r_), lambda k: (0, 0, at(k), 0)),
            pl.BlockSpec((2 * out_rows, held), lambda k: (0, 0)),
            pl.BlockSpec((3 * r_, 2 * r_), lambda k: (0, 0)),
            pl.BlockSpec((1, r_), lambda k: (0, 0)),
        ],
        out_specs=[
            pl.BlockSpec((3, s_, TILE, r_), lambda k: (0, 0, at(k), 0)),
            pl.BlockSpec((s_, TILE, r_), lambda k: (0, at(k), 0)),
        ],
        out_shape=[
            jax.ShapeDtypeStruct(velocity.shape, jnp.float32),
            jax.ShapeDtypeStruct(velocity.shape[1:], jnp.float32),
        ],
        scratch_shapes=[slab] * 7
        + [pltpu.VMEM((held, TILE * r_), jnp.bfloat16)] * 2
        + [pltpu.VMEM((2 * TILE, out_rows, r_), jnp.float32)] * 2
        + [pltpu.VMEM((out_rows * TILE, r_), jnp.float32)] * 3,
        compiler_params=pltpu.CompilerParams(vmem_limit_bytes=56 << 20),
        name="project",
    )(s_ext, pack_l, pack_r, velocity, table, back, rates)


def wall_call(s_ext, pack_l, pack_r, station_of, wall_index, basis, stations):
    wide, tall, r_ = s_ext.shape
    s_ = tall - TILE
    t_ = wide - 2 * TILE
    rows = s_ + 2 * TILE
    steps = wide // TILE
    pitch = rows + (-rows) % r_
    table = np.pad(wall_table(s_), ((0, 0), (0, 0), (0, pitch - rows))).transpose(1, 0, 2).reshape(s_, ORDER * pitch)
    top = table.astype(jnp.bfloat16)
    rest = (table - top.astype(np.float32)).astype(jnp.bfloat16)
    table = jnp.asarray(np.concatenate([top, rest], 0))
    early = stations <= s_
    groups = stations if early else s_
    chosen = station_of if early else jnp.arange(s_, dtype=jnp.int32)
    modes = jnp.asarray(radial_modes(r_)[:WALL_SPAN].astype(np.float32))
    pick = (wall_index[:, None] == jnp.arange(WALL_SPAN)[None, :]).astype(jnp.float32)
    values = jnp.dot(pick, modes, precision=PRECISE)
    rates = jnp.asarray(radial_rates(r_))[None, :]
    tall_rows = ORDER * groups

    def kernel(s_in, near, far, tab, station, rate, value, base, out, parts, high, low, terms, old, new):
        k = pl.program_id(0)

        @pl.when(k == 0)
        def _():
            pick = (lax.broadcasted_iota(jnp.int32, (groups, s_), 0) == station[...]).astype(jnp.bfloat16)
            whole = jnp.dot(jnp.concatenate([pick, pick], axis=1), tab[...], preferred_element_type=jnp.float32)
            for j in range(ORDER):
                top, rest = split(whole[:, j * pitch : j * pitch + rows])
                parts[j * groups : (j + 1) * groups] = top
                parts[tall_rows + j * groups : tall_rows + (j + 1) * groups] = rest

        for i in range(TILE):
            own = s_in[i]
            before, at_low, at_high, after = slab_parts(own, near[i], far[i], s_)
            slab = jnp.concatenate(
                [before, own[:TILE] + at_low]
                + ([own[TILE : s_ - TILE]] if s_ > 2 * TILE else [])
                + [own[s_ - TILE : s_] + at_high, after],
                0,
            )
            top, rest = split(slab)
            high[:, i * r_ : (i + 1) * r_] = top
            low[:, i * r_ : (i + 1) * r_] = rest
        one = jnp.dot(parts[...], high[...], preferred_element_type=jnp.float32)
        two = jnp.dot(parts[:tall_rows], low[...], preferred_element_type=jnp.float32)
        terms[k] = one[:tall_rows] + one[tall_rows:] + two

        @pl.when(k == steps - 1)
        def _():
            zero = jnp.zeros((groups, r_), jnp.float32)
            for ref in (old, new):
                ref[0] = zero
                ref[wide + 1] = zero
            first = (ORDER - 1) * groups

            def start(c, _):
                for i in range(TILE):
                    old[c * TILE + i + 1] = terms[c, first : first + groups, i * r_ : (i + 1) * r_]
                return 0

            lax.fori_loop(0, steps, start, 0)
            source, target = old, new
            for j in range(ORDER - 2, -1, -1):

                def level(c, _, j=j, source=source, target=target):
                    for i in range(TILE):
                        t = c * TILE + i + 1
                        target[t] = (
                            source[t - 1]
                            + source[t + 1]
                            + rate[...] * source[t]
                            + terms[c, j * groups : (j + 1) * groups, i * r_ : (i + 1) * r_]
                        )
                    return 0

                lax.fori_loop(0, steps, level, 0)
                source, target = target, source
            ones = jnp.ones((2 * r_, NA), jnp.bfloat16)

            def gather(c, total):
                for i in range(TILE):
                    t = c * TILE + i
                    product = source[t + LEAD + 1] * value[pl.ds(t, 1), :]
                    top, rest = split(product)
                    sums = jnp.dot(
                        jnp.concatenate([top, rest], axis=1), ones, preferred_element_type=jnp.float32
                    )
                    total = total + sums * base[pl.ds(t, 1), :]
                return total

            out[...] = lax.fori_loop(0, t_ // TILE, gather, jnp.zeros((groups, NA), jnp.float32))

    tile = pl.pallas_call(
        kernel,
        grid=(steps,),
        in_specs=[
            pl.BlockSpec((TILE, tall, r_), lambda k: (k, 0, 0)),
            pl.BlockSpec((TILE, TILE, r_), lambda k: (k, 0, 0)),
            pl.BlockSpec((TILE, TILE, r_), lambda k: (k, 0, 0)),
            pl.BlockSpec((2 * s_, ORDER * pitch), lambda k: (0, 0)),
            pl.BlockSpec((1, s_), lambda k: (0, 0)),
            pl.BlockSpec((1, r_), lambda k: (0, 0)),
            pl.BlockSpec((t_, r_), lambda k: (0, 0)),
            pl.BlockSpec((t_, NA), lambda k: (0, 0)),
        ],
        out_specs=pl.BlockSpec((groups, NA), lambda k: (0, 0)),
        out_shape=jax.ShapeDtypeStruct((groups, NA), jnp.float32),
        scratch_shapes=[
            pltpu.VMEM((2 * tall_rows, rows), jnp.bfloat16),
            pltpu.VMEM((rows, TILE * r_), jnp.bfloat16),
            pltpu.VMEM((rows, TILE * r_), jnp.bfloat16),
            pltpu.VMEM((steps, tall_rows, TILE * r_), jnp.float32),
            pltpu.VMEM((wide + 2, groups, r_), jnp.float32),
            pltpu.VMEM((wide + 2, groups, r_), jnp.float32),
        ],
        compiler_params=pltpu.CompilerParams(vmem_limit_bytes=56 << 20),
        name="wall",
    )(s_ext, pack_l, pack_r, table, chosen[None, :], rates, values, basis)
    if not early:
        select = (station_of[:, None] == jnp.arange(stations)[None, :]).astype(jnp.float32)
        tile = jnp.dot(select.T, tile, precision=PRECISE)
    return tile


def azimuth_basis(first_cell, cells, total):
    column = jnp.arange(NA)
    upper = column >= NA // 2
    harmonic = jnp.where(upper, column - NA // 2 + 1, column)
    index = first_cell + jnp.arange(cells)
    phase = index[:, None] * harmonic[None, :] % total
    angle = 2.0 * math.pi / total * phase.astype(jnp.float32)
    return jnp.where(upper[None, :], jnp.sin(angle), jnp.cos(angle))


def bin_weights(scale):
    column = jnp.arange(NF)
    upper = column >= NF // 2
    harmonic = jnp.where(upper, column - NF // 2 + 1, column)
    phase = jnp.arange(NBIN)[:, None] * harmonic[None, :] % NBIN
    angle = 2.0 * math.pi / NBIN * phase.astype(jnp.float32)
    return jnp.where(upper[None, :], jnp.sin(angle), jnp.cos(angle)) * scale


def send(x, spans, planes, by_span, by_plane):
    pairs = []
    for i in range(spans):
        for j in range(planes):
            to = ((i + by_span) % spans) * planes + (j + by_plane) % planes
            pairs.append((i * planes + j, to))
    return lax.ppermute(x, ("span", "plane"), pairs)


def exchange(s_ext, zr, zl, spans, planes, span_cells, theta_cells):
    edge = ORDER + 1
    first = LEAD - 1
    last = LEAD + theta_cells - ORDER
    after = LEAD - ORDER
    before = LEAD + theta_cells - 1

    def planes_of(z, step):
        mid = send(z, spans, planes, step, 0)
        low = send(z[last : last + edge], spans, planes, step, 1)
        high = send(z[first : first + edge], spans, planes, step, -1)
        total = mid.shape[0]
        low = jnp.pad(low, ((after, total - after - edge), (0, 0), (0, 0)))
        high = jnp.pad(high, ((before, total - before - edge), (0, 0), (0, 0)))
        return mid + low + high

    low = send(s_ext[last : last + edge], spans, planes, 0, 1)
    high = send(s_ext[first : first + edge], spans, planes, 0, -1)
    from_left = planes_of(zr, 1)
    from_right = planes_of(zl, -1)
    hop = 1
    while hop < spans and np.any(hop_table(hop * span_cells)):
        table = hop_table(hop * span_cells)
        left_table = np.zeros((TILE, TILE), np.float32)
        left_table[: TILE - ORDER - 1 : -1, [0, 7, 6, 5, 4, 3]] = table
        right_table = np.zeros((TILE, TILE), np.float32)
        right_table[:ORDER, [7, 0, 1, 2, 3, 4]] = table
        far_left = planes_of(zr, hop + 1)
        far_right = planes_of(zl, -hop - 1)
        from_left = from_left + jnp.einsum("bd,adr->abr", left_table, far_left, precision=PRECISE)
        from_right = from_right + jnp.einsum("bd,adr->abr", right_table, far_right, precision=PRECISE)
        hop += 1
    s_ext = s_ext.at[after : after + edge].add(low).at[before : before + edge].add(high)
    return s_ext, from_left, from_right


def share(rows, spans, planes):
    each = rows.shape[0]
    here = lax.axis_index("plane")
    whole = jnp.zeros((planes,) + rows.shape, rows.dtype)
    order = jnp.arange(planes)[:, None, None]
    for step in range(planes):
        piece = rows if step == 0 else send(rows, spans, planes, 0, step)
        whole = jnp.where(order == (here - step) % planes, piece[None], whole)
    return whole.reshape(planes * each, rows.shape[1])


def local(velocity, wall_history, phase_bin, station_of, wall_index, spans, planes):
    _, span_cells, theta_cells, _ = velocity.shape
    total_theta = theta_cells * planes
    stations = ST_DEV * spans
    basis = azimuth_basis(lax.axis_index("plane") * theta_cells, theta_cells, total_theta)
    s_ext, zr, zl = source_call(velocity)
    tiles = bins_call(wall_history, phase_bin, station_of, basis, stations)
    s_ext, pack_l, pack_r = exchange(s_ext, zr, zl, spans, planes, span_cells, theta_cells)
    wall = wall_call(s_ext, pack_l, pack_r, station_of, wall_index, basis, stations)
    newest = (jnp.arange(NBIN) == phase_bin[-1]).astype(jnp.float32)
    tiles = tiles + newest[None, :, None] * wall[:, None, :]
    each = stations // (spans * planes)
    parts = lax.all_to_all(tiles, ("span", "plane"), split_axis=0, concat_axis=0, tiled=True)
    corrected, pressure = project_call(s_ext, pack_l, pack_r, velocity)
    parts, pressure = lax.optimization_barrier((parts, pressure))
    held = jnp.sum(parts.reshape(spans * planes, each, NBIN, NA), axis=0)
    weights = bin_weights(1.0 / math.sqrt(total_theta * (wall_history.shape[0] + 1)))
    mine = jnp.einsum("sba,bf->saf", held, weights, precision=PRECISE).reshape(each, NA * NF)
    coefficients = share(mine, spans, planes)
    return corrected, pressure, coefficients


def solution(mesh):
    spans = mesh.shape["span"]
    planes = mesh.shape["plane"]
    in_specs = (
        P(None, "span", "plane", None),
        P(None, "span", "plane"),
        P(),
        P("span"),
        P("plane"),
    )
    out_specs = (P(None, "span", "plane", None), P("span", "plane", None), P("span", None))

    def body(*args):
        return local(*args, spans, planes)

    return jax.shard_map(body, mesh=mesh, in_specs=in_specs, out_specs=out_specs, check_vma=False)
```

time: 264 us -> 159 us (0.60)
  blocking collectives: 40.8 us -> 0 us
  Pallas kernels: 150 us -> 110 us
  waiting for transfers between devices: 27.4 us -> 11.5 us
  between operations: 14.9 us -> 0.85 us
  starting transfers between devices: 13.3 us -> 21.5 us
    pallas_call x1, Pallas kernels: 106 us -> 52 us  [project_call(): pl.pallas_call(kernel, grid=(steps,), in_specs=[pl.BlockSpec((TILE, s_ +...]
    unnamed x1 -> x0, blocking collectives: 35.1 us -> none
    psum x1 -> x0, waiting for transfers between devices: 23.1 us -> none  [local(): held = lax.psum(held, 'plane')]
    pallas_call x1 -> x2, Pallas kernels: 27.5 us -> 46.6 us  [the longest x1 25.6 us: source_call(): pl.pallas_call(body, grid=(wide // TILE,), in_specs=[part(0), part(1), pa...]
    ppermute x8 -> x11, waiting for transfers between devices: 4.27 us -> 11.5 us  [send(): return lax.ppermute(x, ('span', 'plane'), pairs)]
    all_to_all x0 -> x1, starting transfers between devices: none -> 7.11 us  [local(): lax.all_to_all(tiles, ('span', 'plane'), split_axis=0, concat_axis=0, til...]
    psum x1 -> x0, blocking collectives: 5.67 us -> none  [local(): lax.psum(lax.psum_scatter(wall_tile, 'span', scatter_dimension=0, tiled=T...]
    reduce_sum x1, other arithmetic: 5.63 us -> 0.07 us  [local(): held = jnp.sum(parts.reshape(spans * planes, each, NBIN, NA), axis=0)]
  transfers between devices with their start and end apart: 10 -> 12, of which waited for: 3 -> 6; matrix products, arithmetic and copies ran while one was open for 5% -> 4% of each run, Pallas kernels for 47% -> 40%
where the time goes in v2:
time: 159 us; the launch traced here: 158 us
  Pallas kernels  110 us (69%)
  starting transfers between devices  21.5 us (14%)
  waiting for transfers between devices  11.5 us (7%)
  other arithmetic  9.23 us (6%)
  local copies, waits for them, and re-layouts  3.46 us (2%)
    pallas_call x1, Pallas kernels, project_call(): pl.pallas_call(kernel, grid=(steps,), in_specs=[pl.BlockSpec((TILE, s_ +...  52 us
    pallas_call x1, Pallas kernels, source_call(): pl.pallas_call(body, grid=(wide // TILE,), in_specs=[part(0), part(1), pa...  25.6 us
    pallas_call x1, Pallas kernels, wall_call(): pl.pallas_call(kernel, grid=(steps,), in_specs=[pl.BlockSpec((TILE, tall,...  21 us
    ppermute x11, starting transfers between devices, send(): return lax.ppermute(x, ('span', 'plane'), pairs)  14.3 us
    pallas_call x1, Pallas kernels, bins_call(): pl.pallas_call(kernel, grid_spec=pltpu.PrefetchScalarGridSpec(num_scalar_...  11.6 us
    ppermute x11, waiting for transfers between devices, send(): return lax.ppermute(x, ('span', 'plane'), pairs)  11.5 us
    all_to_all x1, starting transfers between devices, local(): lax.all_to_all(tiles, ('span', 'plane'), split_axis=0, concat_axis=0, til...  7.11 us
  transfers between devices with their start and end apart: 12, of which 6 were waited for; matrix products, arithmetic and copies ran while one was open for 4% of the time, Pallas kernels for 40%

profile of v2, /device:TPU:0, one launch (start us, length us, event | category | flops | bytes accessed | tf_op | source)
XLA Modules:
  0.0 158.0 jit_solution(8924994819927992613)
XLA Ops:
  0.6 0.0 copy-start.1
  0.6 0.9 copy-done.1
  1.6 0.0 copy-start.2
  1.6 0.7 copy-done.2
  2.3 0.0 copy-start.4
  2.3 0.0 copy-start.3
  2.3 25.6 %source.1 = (f32[144,136,128]{2,1,0:T(8,128)}, f32[144,8,128]{2,1,0:T(8,128)S(1)}, f32[144,8,128]{2,1,0:T(8,128)S(1)}) custom-call(f32[3,128,128,128]{3,2,1,0:T(8,128)} %v.1, f32[3,128,128,128]{3,2,1,0:T(8,128)} %v.1, f32[3,128,128,128]{3,2,1,0:T(8,128)} %v.1, bf16[32,128]{1,0:T(8,128)(2,1)S(1)} %copy-done.2, bf16[768,128]{1,0:T(8,128)(2,1)S(1)} %copy-done.1), custom_call_target="tpu_custom_call" | custom-call | tf_op jit(solution)/shard_map/source/pallas_call | solution.py:178
  27.9 0.0 copy-start.5
  27.9 0.0 copy-start.6
  27.9 1.1 slice.70
  28.9 0.5 collective-permute-start
  29.5 5.6 %collective-permute-start.5 = (f32[144,8,128]{2,1,0:T(8,128)S(1)}, f32[144,8,128]{2,1,0:T(8,128)S(1)}, u32[]{:S(2)}, u32[]{:S(2)}) collective-permute-start(f32[144,8,128]{2,1,0:T(8,128)S(1)} %get-tuple-element.36), channel_id=1, source_target_pairs={{0,28},{1,29},{2,30},{3,31},{4,0},{5,1},{6,2},{7,3},{8,4},{9,5},{1... | collective-permute-start | bytes 1769480 | tf_op jit(solution)/shard_map/ppermute | solution.py:552
  35.0 1.4 collective-permute-start.6
  36.5 1.1 collective-permute-start.7
  37.6 0.7 collective-permute-start.2
  38.3 0.3 cosine_select_fusion.base
  38.6 0.0 copy-done.4
  38.6 0.0 copy-start
  38.6 0.6 slice.77
  39.2 0.0 copy-done.3
  39.2 11.6 %bins.2 = f32[2048,128]{1,0:T(8,128)S(1)} custom-call(s32[256]{0:T(256)S(1)} %copy-done.4, f32[255,128,128]{2,1,0:T(8,128)} %x.9, s32[1,128]{1,0:T(1,128)S(1)} %bitcast.10, f32[128,128]{1,0:T(8,128)S(1)} %cosine_select_fusion.base), custom_call_target="tpu_custom_call" | custom-call | tf_op jit(solution)/shard_map/bins/pallas_call | solution.py:248
  50.9 0.0 copy-done.5
  50.9 0.0 copy-done.6
  50.9 0.9 fusion.4.value
  51.8 0.6 compare_convert_fusion
  52.4 0.0 collective-permute-done
  52.4 2.1 %collective-permute-start.3 = (f32[6,8,128]{2,1,0:T(8,128)S(1)}, f32[6,8,128]{2,1,0:T(8,128)S(1)}, u32[]{:S(2)}, u32[]{:S(2)}) collective-permute-start(f32[6,8,128]{2,1,0:T(8,128)S(1)} %get-tuple-element.45), channel_id=1, source_target_pairs={{0,5},{1,6},{2,7},{3,4},{4,9},{5,10},{6,11},{7,8},{8,13},{9,14},{1... | collective-permute-start | bytes 73736 | tf_op jit(solution)/shard_map/ppermute | solution.py:552
  54.5 2.0 %fusion.32 = (f32[6,136,128]{2,1,0:T(8,128)S(1)}, f32[144,136,128]{2,1,0:T(8,128)}) fusion(f32[144,136,128]{2,1,0:T(8,128)} %get-tuple-element.34, f32[6,136,128]{2,1,0:T(8,128)S(1)} %collective-permute-done), kind=kLoop, calls=%fused_computation.55 | loop fusion | flops 104448 | bytes 2088960 | tf_op jit(solution)/shard_map/slice | solution.py:572
  56.5 3.6 %collective-permute-done.6 = f32[6,8,128]{2,1,0:T(8,128)S(1)} collective-permute-done((f32[6,8,128]{2,1,0:T(8,128)S(1)}, f32[6,8,128]{2,1,0:T(8,128)S(1)}, u32[]{:S(2)}, u32[]{:S(2)}) %collective-permute-start.6) | collective-permute-done | bytes 24608 | tf_op jit(solution)/shard_map/ppermute | solution.py:552
  60.1 0.0 collective-permute-start.4
  60.1 0.3 collective-permute-done.7
  60.4 0.8 collective-permute-start.1
  61.3 0.0 collective-permute-done.5
  61.3 0.9 pad_add_fusion.far
  62.1 0.0 copy-done
  62.1 0.0 collective-permute-done.3
  62.1 3.9 %collective-permute-done.4 = f32[6,8,128]{2,1,0:T(8,128)S(1)} collective-permute-done((f32[6,8,128]{2,1,0:T(8,128)S(1)}, f32[6,8,128]{2,1,0:T(8,128)S(1)}, u32[]{:S(2)}, u32[]{:S(2)}) %collective-permute-start.4) | collective-permute-done | bytes 24608 | tf_op jit(solution)/shard_map/ppermute | solution.py:552
  66.0 0.0 collective-permute-done.2
  66.0 0.8 pad_add_fusion.1.near
  66.9 0.2 collective-permute-done.1
  67.1 1.8 %fusion.s_in = f32[144,136,128]{2,1,0:T(8,128)} fusion(f32[144,136,128]{2,1,0:T(8,128)} %get-tuple-element.42, f32[6,136,128]{2,1,0:T(8,128)S(1)} %collective-permute-done.1), kind=kLoop, calls=%fused_computation.4 | loop fusion | flops 104448 | bytes 1253376 | tf_op jit(solution)/shard_map/scatter-add | solution.py:587
  68.9 21.0 %wall.1 = f32[32,128]{1,0:T(8,128)} custom-call(f32[144,136,128]{2,1,0:T(8,128)} %fusion.s_in, f32[144,8,128]{2,1,0:T(8,128)} %pad_add_fusion.1.near, f32[144,8,128]{2,1,0:T(8,128)} %pad_add_fusion.far, bf16[256,1280]{1,0:T(8,128)(2,1)} %constant.161.clone.tab, s32[1,128]{1,0:T(1,128)} %bitcast.9, f32[1,128]{1,0:T(1,128)} %constant.174.rate, ...), custom_call_target="tpu_custom_call" | custom-call | tf_op jit(solution)/shard_map/wall/pallas_call | solution.py:495
  89.9 1.9 %multiply_add_fusion = f32[32,64,128]{2,1,0:T(8,128)} fusion(f32[32,64,128]{2,1,0:T(8,128)S(1)} %bitcast.8, f32[32,128]{1,0:T(8,128)} %wall.1, f32[64]{0:T(128)S(1)} %compare_convert_fusion), kind=kLoop, calls=%fused_computation | loop fusion | flops 524288 | bytes 2113792 | tf_op jit(solution)/shard_map/add | solution.py:612
  91.8 7.1 %all-to-all-start = ((f32[32,64,128]{2,1,0:T(8,128)}), f32[32,64,128]{2,1,0:T(8,128)S(1)}, u32[]{:S(2)}, u32[]{:S(2)}) async-start(f32[32,64,128]{2,1,0:T(8,128)} %multiply_add_fusion), calls=%async_computation | async-start | bytes 2097152 | tf_op jit(solution)/shard_map/all_to_all | solution.py:614
  99.0 52.0 %project.1 = (f32[3,128,128,128]{3,2,1,0:T(8,128)}, f32[128,128,128]{2,1,0:T(8,128)}) custom-call(f32[144,136,128]{2,1,0:T(8,128)} %fusion.s_in, f32[144,8,128]{2,1,0:T(8,128)} %pad_add_fusion.1.near, f32[144,8,128]{2,1,0:T(8,128)} %pad_add_fusion.far, f32[3,128,128,128]{3,2,1,0:T(8,128)} %v.1, bf16[272,160]{1,0:T(8,128)(2,1)} %constant.164.clone.tab, ...), custom_call_target="tpu_custom_call" | custom-call | tf_op jit(solution)/shard_map/project/pallas_call | solution.py:373
  151.0 0.0 all-to-all-done
  151.0 0.1 reduce_sum.9
  151.1 0.3 fusion.8
  151.5 0.1 reshape.205
  151.6 1.5 collective-permute-start.8
  153.1 0.4 collective-permute-start.9
  153.5 0.2 collective-permute-start.10
  153.7 0.1 broadcast_in_dim.112
  153.7 1.0 collective-permute-done.8
  154.7 2.4 %collective-permute-done.9 = f32[1,8192]{1,0:T(1,128)S(1)} collective-permute-done((f32[1,8192]{1,0:T(1,128)S(1)}, f32[1,8192]{1,0:T(1,128)S(1)}, u32[]{:S(2)}, u32[]{:S(2)}) %collective-permute-start.9) | collective-permute-done | bytes 32800 | tf_op jit(solution)/shard_map/ppermute | solution.py:552
  157.2 0.0 collective-permute-done.10
  157.2 0.8 select_select_fusion
  (8 shorter events, 0.0 us)
Async XLA Ops:
  0.6 0.9 copy-start.1
  1.6 0.7 copy-start.2
  2.3 36.4 %copy-start.4 = (s32[256]{0:T(256)S(1)}, s32[256]{0:T(256)}, u32[]{:S(2)}) copy-start(s32[256]{0:T(256)} %bins.3) | copy-start | bytes 3076
  2.3 37.0 %copy-start.3 = (s32[128]{0:T(128)S(1)}, s32[128]{0:T(128)}, u32[]{:S(2)}) copy-start(s32[128]{0:T(128)} %param.20) | copy-start | bytes 1540
  27.9 23.0 %copy-start.5 = (f32[8,128]{1,0:T(8,128)S(1)}, f32[8,128]{1,0:T(8,128)}, u32[]{:S(2)}) copy-start(f32[8,128]{1,0:T(8,128)} %constant.162.clone) | copy-start | bytes 12292
  27.9 23.0 %copy-start.6 = (s32[128]{0:T(128)S(1)}, s32[128]{0:T(128)}, u32[]{:S(2)}) copy-start(s32[128]{0:T(128)} %param.21) | copy-start | bytes 1540
  28.9 23.5 %collective-permute-start = (f32[6,136,128]{2,1,0:T(8,128)S(1)}, f32[6,136,128]{2,1,0:T(8,128)S(1)}, u32[]{:S(2)}, u32[]{:S(2)}) collective-permute-start(f32[6,136,128]{2,1,0:T(8,128)S(1)} %slice.70), channel_id=1, source_target_pairs={{0,1},{1,2},{2,3},{3,0},{4,5},{5,6},{6,7},{7,4},{8,9},{9,10},{10,1... | collective-permute-start | bytes 1253384 | tf_op jit(solution)/shard_map/ppermute | solution.py:552
  29.5 31.8 %collective-permute-start.5 = (f32[144,8,128]{2,1,0:T(8,128)S(1)}, f32[144,8,128]{2,1,0:T(8,128)S(1)}, u32[]{:S(2)}, u32[]{:S(2)}) collective-permute-start(f32[144,8,128]{2,1,0:T(8,128)S(1)} %get-tuple-element.36), channel_id=1, source_target_pairs={{0,28},{1,29},{2,30},{3,31},{4,0},{5,1},{6,2},{7,3},{8,4},{9,5},{1... | collective-permute-start | bytes 1769480 | tf_op jit(solution)/shard_map/ppermute | solution.py:552
  35.0 25.0 %collective-permute-start.6 = (f32[6,8,128]{2,1,0:T(8,128)S(1)}, f32[6,8,128]{2,1,0:T(8,128)S(1)}, u32[]{:S(2)}, u32[]{:S(2)}) collective-permute-start(f32[6,8,128]{2,1,0:T(8,128)S(1)} %get-tuple-element.43), channel_id=1, source_target_pairs={{0,29},{1,30},{2,31},{3,28},{4,1},{5,2},{6,3},{7,0},{8,5},{9,6},{1... | collective-permute-start | bytes 73736 | tf_op jit(solution)/shard_map/ppermute | solution.py:552
  36.5 23.9 %collective-permute-start.7 = (f32[6,8,128]{2,1,0:T(8,128)S(1)}, f32[6,8,128]{2,1,0:T(8,128)S(1)}, u32[]{:S(2)}, u32[]{:S(2)}) collective-permute-start(f32[6,8,128]{2,1,0:T(8,128)S(1)} %get-tuple-element.44), channel_id=1, source_target_pairs={{0,31},{1,28},{2,29},{3,30},{4,3},{5,0},{6,1},{7,2},{8,7},{9,4},{1... | collective-permute-start | bytes 73736 | tf_op jit(solution)/shard_map/ppermute | solution.py:552
  37.6 28.5 %collective-permute-start.2 = (f32[144,8,128]{2,1,0:T(8,128)S(1)}, f32[144,8,128]{2,1,0:T(8,128)S(1)}, u32[]{:S(2)}, u32[]{:S(2)}) collective-permute-start(f32[144,8,128]{2,1,0:T(8,128)S(1)} %get-tuple-element.35), channel_id=1, source_target_pairs={{0,4},{1,5},{2,6},{3,7},{4,8},{5,9},{6,10},{7,11},{8,12},{9,13},{1... | collective-permute-start | bytes 1769480 | tf_op jit(solution)/shard_map/ppermute | solution.py:552
  38.6 23.5 %copy-start = (f32[128,128]{1,0:T(8,128)}, f32[128,128]{1,0:T(8,128)S(1)}, u32[]{:S(2)}) copy-start(f32[128,128]{1,0:T(8,128)S(1)} %cosine_select_fusion.base) | copy-start | bytes 196612
  52.4 9.7 %collective-permute-start.3 = (f32[6,8,128]{2,1,0:T(8,128)S(1)}, f32[6,8,128]{2,1,0:T(8,128)S(1)}, u32[]{:S(2)}, u32[]{:S(2)}) collective-permute-start(f32[6,8,128]{2,1,0:T(8,128)S(1)} %get-tuple-element.45), channel_id=1, source_target_pairs={{0,5},{1,6},{2,7},{3,4},{4,9},{5,10},{6,11},{7,8},{8,13},{9,14},{1... | collective-permute-start | bytes 73736 | tf_op jit(solution)/shard_map/ppermute | solution.py:552
  60.1 5.9 %collective-permute-start.4 = (f32[6,8,128]{2,1,0:T(8,128)S(1)}, f32[6,8,128]{2,1,0:T(8,128)S(1)}, u32[]{:S(2)}, u32[]{:S(2)}) collective-permute-start(f32[6,8,128]{2,1,0:T(8,128)S(1)} %get-tuple-element.46), channel_id=1, source_target_pairs={{0,7},{1,4},{2,5},{3,6},{4,11},{5,8},{6,9},{7,10},{8,15},{9,12},{1... | collective-permute-start | bytes 73736 | tf_op jit(solution)/shard_map/ppermute | solution.py:552
  60.4 6.7 %collective-permute-start.1 = (f32[6,136,128]{2,1,0:T(8,128)S(1)}, f32[6,136,128]{2,1,0:T(8,128)S(1)}, u32[]{:S(2)}, u32[]{:S(2)}) collective-permute-start(f32[6,136,128]{2,1,0:T(8,128)S(1)} %get-tuple-element.41), channel_id=1, source_target_pairs={{0,3},{1,0},{2,1},{3,2},{4,7},{5,4},{6,5},{7,6},{8,11},{9,8},{10,9... | collective-permute-start | bytes 1253384 | tf_op jit(solution)/shard_map/ppermute | solution.py:552
  91.8 59.3 %all-to-all-start = ((f32[32,64,128]{2,1,0:T(8,128)}), f32[32,64,128]{2,1,0:T(8,128)S(1)}, u32[]{:S(2)}, u32[]{:S(2)}) async-start(f32[32,64,128]{2,1,0:T(8,128)} %multiply_add_fusion), calls=%async_computation | async-start | bytes 2097152 | tf_op jit(solution)/shard_map/all_to_all | solution.py:614
  151.6 3.2 %collective-permute-start.8 = (f32[1,8192]{1,0:T(1,128)S(1)}, f32[1,8192]{1,0:T(1,128)S(1)}, u32[]{:S(2)}, u32[]{:S(2)}) collective-permute-start(f32[1,8192]{1,0:T(1,128)S(1)} %reshape.205), channel_id=1, source_target_pairs={{0,3},{1,0},{2,1},{3,2},{4,7},{5,4},{6,5},{7,6},{8,11},{9,8},{10,9... | collective-permute-start | bytes 98312 | tf_op jit(solution)/shard_map/ppermute | solution.py:552
  153.1 4.1 %collective-permute-start.9 = (f32[1,8192]{1,0:T(1,128)S(1)}, f32[1,8192]{1,0:T(1,128)S(1)}, u32[]{:S(2)}, u32[]{:S(2)}) collective-permute-start(f32[1,8192]{1,0:T(1,128)S(1)} %reshape.205), channel_id=1, source_target_pairs={{0,2},{1,3},{2,0},{3,1},{4,6},{5,7},{6,4},{7,5},{8,10},{9,11},{10,... | collective-permute-start | bytes 98312 | tf_op jit(solution)/shard_map/ppermute | solution.py:552
  153.5 3.7 %collective-permute-start.10 = (f32[1,8192]{1,0:T(1,128)S(1)}, f32[1,8192]{1,0:T(1,128)S(1)}, u32[]{:S(2)}, u32[]{:S(2)}) collective-permute-start(f32[1,8192]{1,0:T(1,128)S(1)} %reshape.205), channel_id=1, source_target_pairs={{0,1},{1,2},{2,3},{3,0},{4,5},{5,6},{6,7},{7,4},{8,9},{9,10},{10,1... | collective-permute-start | bytes 98312 | tf_op jit(solution)/shard_map/ppermute | solution.py:552

commit v3 on v2

--- a/solution.py
+++ b/solution.py
@@ -80,17 +80,24 @@
     entries = [inverse_entry(d) for d in range(cells + 2 * TILE)]
     for i in range(cells + 2):
         for z in range(-ORDER - ITERS, cells + ORDER + ITERS):
-            table[i, (z + TILE) % rows] = entries[abs(i - 1 - z)]
+            table[(i - 1) % (cells + TILE), (z + TILE) % rows] = entries[abs(i - 1 - z)]
     return representable(table)
 
 
-def wall_table(cells):
-    table = np.zeros((ORDER, cells, cells + 2 * TILE))
+def wall_hops(cells):
+    hops = 1
+    while representable([inverse_entry(hops * cells, j + 1) for j in range(ORDER)]).any():
+        hops += 1
+    return hops
+
+
+def wall_table(cells, hops):
+    table = np.zeros(((2 * hops + 1) * cells, ORDER, cells + TILE))
     for j in range(ORDER):
-        entries = [inverse_entry(d, j + 1) for d in range(cells + ORDER)]
-        for i in range(cells):
-            for z in range(-ORDER, cells + ORDER):
-                table[j, i, z + TILE] = entries[abs(i - z)]
+        entries = np.array([inverse_entry(d, j + 1) for d in range((hops + 1) * cells + 2)])
+        targets = np.arange((2 * hops + 1) * cells) - hops * cells
+        for z in range(-1, cells + 1):
+            table[:, j, z % (cells + TILE)] = entries[np.abs(targets - z)]
     return representable(table)
 
 
@@ -289,8 +296,10 @@
     rates = jnp.asarray(radial_rates(r_))[None, :]
     slots = TILE + 2
 
-    def kernel(s_in, near, far, v, tab, turn, rate, corrected, pressure, *scratch):
-        a0, a1, a2, a3, w1, w2, w3, high, low, pot, rad, pn, gn, rn = scratch
+    share_ = TILE // ITERS
+
+    def kernel(s_in, near, far, v0, v1, v2, tab, turn, rate, c0, c1, c2, pressure, *scratch):
+        a0, a1, a2, a3, w1, w2, w3, high, low, ready_high, ready_low, pot, rad = scratch
         k = pl.program_id(0)
         levels_a = [a0, a1, a2, a3]
         levels_w = [a0, w1, w2, w3]
@@ -300,30 +309,35 @@
             for ref in (a0, a1, a2, a3, w1, w2, w3):
                 ref[TILE:slots] = jnp.zeros((2, rows, r_), jnp.float32)
             a0[:, rows - TILE :] = jnp.zeros((slots, TILE, r_), jnp.float32)
-            pot[TILE:] = jnp.zeros((TILE, out_rows, r_), jnp.float32)
-            rad[TILE:] = jnp.zeros((TILE, out_rows, r_), jnp.float32)
+            high[...] = jnp.zeros_like(high)
+            low[...] = jnp.zeros_like(low)
+            pot[...] = jnp.zeros_like(pot)
+            rad[...] = jnp.zeros_like(rad)
 
         for ref in (a0, a1, a2, a3, w1, w2, w3):
             ref[0:2] = ref[TILE:slots]
         pot[:TILE] = pot[TILE:]
         rad[:TILE] = rad[TILE:]
-
-        def load(i, _):
+        ready_high[...] = high[...]
+        ready_low[...] = low[...]
+
+        for i in range(TILE):
             own = s_in[i]
             before, at_low, at_high, after = slab_parts(own, near[i], far[i], s_)
             a0[i + 2, 0:TILE] = before
-            a0[i + 2, TILE : TILE + s_] = own[:s_]
-            a0[i + 2, TILE : 2 * TILE] += at_low
-            a0[i + 2, s_ : s_ + TILE] += at_high
+            a0[i + 2, TILE : 2 * TILE] = own[:TILE] + at_low
+            if s_ > 2 * TILE:
+                a0[i + 2, 2 * TILE : s_] = own[TILE : s_ - TILE]
+            a0[i + 2, s_ : s_ + TILE] = own[s_ - TILE : s_] + at_high
             a0[i + 2, s_ + TILE : s_ + 2 * TILE] = after
-            return 0
-
-        lax.fori_loop(0, TILE, load, 0)
 
         for n in range(1, ITERS + 1):
             past, weighted = levels_a[n - 1], levels_w[n - 1]
-
-            def sweep(i, _, n=n, past=past, weighted=weighted):
+            columns = slice((n - 1) * share_ * r_, n * share_ * r_)
+            one = jnp.dot(tab[...], ready_high[:, columns], preferred_element_type=jnp.float32)
+            two = jnp.dot(tab[:out_rows], ready_low[:, columns], preferred_element_type=jnp.float32)
+            solved = one[:out_rows] + one[out_rows:] + two
+            for i in range(TILE):
                 total = past[i] + past[i + 2] + rate[...] * past[i + 1]
                 mid = weighted[i + 1]
                 value = 6.0 * mid - (pltpu.roll(mid, 1, 0) + pltpu.roll(mid, rows - 1, 0)) + total
@@ -333,50 +347,41 @@
                 else:
                     value = jnp.concatenate([value, jnp.zeros((held - rows, r_), jnp.float32)], 0)
                     top_part, rest_part = split(value)
-                    at = pl.multiple_of(i * r_, r_)
-                    high[:, pl.ds(at, r_)] = top_part
-                    low[:, pl.ds(at, r_)] = rest_part
-                return 0
-
-            lax.fori_loop(0, TILE, sweep, 0)
-
-        one = jnp.dot(tab[...], high[...], preferred_element_type=jnp.float32)
-        two = jnp.dot(tab[:out_rows], low[...], preferred_element_type=jnp.float32)
-        total = one[:out_rows] + one[out_rows:] + two
-        for i in range(TILE):
-            here = jnp.dot(triple(total[:, i * r_ : (i + 1) * r_]), turn[...], preferred_element_type=jnp.float32)
-            pot[TILE + i] = here[:, :r_]
-            rad[TILE + i] = here[:, r_:]
-
-        @pl.when(k >= 2)
-        def _():
-            for i in range(TILE):
+                    high[:, i * r_ : (i + 1) * r_] = top_part
+                    low[:, i * r_ : (i + 1) * r_] = rest_part
+            solved = jnp.concatenate([solved[:, i * r_ : (i + 1) * r_] for i in range(share_)], 0)
+            solved = jnp.dot(triple(solved), turn[...], preferred_element_type=jnp.float32)
+            for i in range(share_):
+                pot[TILE + (n - 1) * share_ + i] = solved[i * out_rows : (i + 1) * out_rows, :r_]
+                rad[TILE + (n - 1) * share_ + i] = solved[i * out_rows : i * out_rows + s_, r_:]
+            for i in range((n - 1) * share_, n * share_):
                 at = LEAD - ORDER + 1 + i
-                pn[pl.ds(i, out_rows, stride=TILE), :] = pot[at]
-                rn[pl.ds(i, out_rows, stride=TILE), :] = rad[at]
-                gn[pl.ds(i, out_rows, stride=TILE), :] = 0.5 * (pot[at + 1] - pot[at - 1])
-
-            def finish(z, _):
-                here = pl.ds(pl.multiple_of((z + 1) * TILE, TILE), TILE)
-                down = pn[pl.ds(pl.multiple_of(z * TILE, TILE), TILE), :]
-                up = pn[pl.ds(pl.multiple_of((z + 2) * TILE, TILE), TILE), :]
-                pressure[z] = pn[here, :]
-                corrected[0, z] = v[0, z] - rn[here, :]
-                corrected[1, z] = v[1, z] - gn[here, :]
-                corrected[2, z] = v[2, z] - 0.5 * (up - down)
-                return 0
-
-            lax.fori_loop(0, s_, finish, 0, unroll=8)
-
-    at = lambda k: jnp.maximum(k - 2, 0)
+                out = pl.ds(i, s_, stride=TILE)
+                mid = pot[at]
+                along = pltpu.roll(mid, out_rows - 1, 0) - pltpu.roll(mid, 1, 0)
+                pressure[out, :] = mid[:s_]
+                c0[out, :] = v0[out, :] - rad[at]
+                c1[out, :] = v1[out, :] - 0.5 * (pot[at + 1, :s_] - pot[at - 1, :s_])
+                c2[out, :] = v2[out, :] - 0.5 * along[:s_]
+
+    def flat(ref):
+        return ref.reshape(s_ * TILE, r_)
+
+    def body(s_in, near, far, v, tab, turn, rate, corrected, pressure, *scratch):
+        parts = [flat(v.at[i]) for i in range(3)]
+        outs = [flat(corrected.at[i]) for i in range(3)]
+        kernel(s_in, near, far, *parts, tab, turn, rate, *outs, flat(pressure), *scratch)
+
+    at = lambda k: jnp.maximum(k - 3, 0)
+    of = lambda k: jnp.minimum(k, steps - 1)
     slab = pltpu.VMEM((slots, rows, r_), jnp.float32)
     return pl.pallas_call(
-        kernel,
-        grid=(steps,),
+        body,
+        grid=(steps + 1,),
         in_specs=[
-            pl.BlockSpec((TILE, s_ + TILE, r_), lambda k: (k, 0, 0)),
-            pl.BlockSpec((TILE, TILE, r_), lambda k: (k, 0, 0)),
-            pl.BlockSpec((TILE, TILE, r_), lambda k: (k, 0, 0)),
+            pl.BlockSpec((TILE, s_ + TILE, r_), lambda k: (of(k), 0, 0)),
+            pl.BlockSpec((TILE, TILE, r_), lambda k: (of(k), 0, 0)),
+            pl.BlockSpec((TILE, TILE, r_), lambda k: (of(k), 0, 0)),
             pl.BlockSpec((3, s_, TILE, r_), lambda k: (0, 0, at(k), 0)),
             pl.BlockSpec((2 * out_rows, held), lambda k: (0, 0)),
             pl.BlockSpec((3 * r_, 2 * r_), lambda k: (0, 0)),
@@ -391,61 +396,70 @@
             jax.ShapeDtypeStruct(velocity.shape[1:], jnp.float32),
         ],
         scratch_shapes=[slab] * 7
-        + [pltpu.VMEM((held, TILE * r_), jnp.bfloat16)] * 2
-        + [pltpu.VMEM((2 * TILE, out_rows, r_), jnp.float32)] * 2
-        + [pltpu.VMEM((out_rows * TILE, r_), jnp.float32)] * 3,
+        + [pltpu.VMEM((held, TILE * r_), jnp.bfloat16)] * 4
+        + [pltpu.VMEM((2 * TILE, out_rows, r_), jnp.float32), pltpu.VMEM((2 * TILE, s_, r_), jnp.float32)],
         compiler_params=pltpu.CompilerParams(vmem_limit_bytes=56 << 20),
         name="project",
     )(s_ext, pack_l, pack_r, velocity, table, back, rates)
 
 
-def wall_call(s_ext, pack_l, pack_r, station_of, wall_index, basis, stations):
+def wall_call(s_ext, near_stations, near_walls, near_basis, stations):
+    cells = s_ext.shape[1] - TILE
+    table = wall_table(cells, wall_hops(cells))
+    targets = near_stations.shape[0]
+    if stations <= targets:
+        return wall_part(s_ext, table, near_stations, near_walls, near_basis, stations)
+    batch = max(d for d in range(TILE, 6 * TILE + 1, TILE) if targets % d == 0)
+    index = jnp.arange(batch, dtype=jnp.int32)
+    planes = [
+        wall_part(s_ext, table[i : i + batch], index, near_walls, near_basis, batch) for i in range(0, targets, batch)
+    ]
+    select = (near_stations[:, None] == jnp.arange(stations)[None, :]).astype(jnp.float32)
+    return jnp.dot(select.T, jnp.concatenate(planes, 0), precision=PRECISE)
+
+
+def wall_part(s_ext, table, chosen, near_walls, near_basis, groups):
     wide, tall, r_ = s_ext.shape
     s_ = tall - TILE
-    t_ = wide - 2 * TILE
-    rows = s_ + 2 * TILE
-    steps = wide // TILE
+    rows = tall + (-tall) % (2 * TILE)
+    chunks = wide // TILE
+    group = max(d for d in range(1, 4) if chunks % d == 0)
+    steps = chunks // group
+    targets = chosen.shape[0]
     pitch = rows + (-rows) % r_
-    table = np.pad(wall_table(s_), ((0, 0), (0, 0), (0, pitch - rows))).transpose(1, 0, 2).reshape(s_, ORDER * pitch)
+    table = np.pad(table, ((0, 0), (0, 0), (0, pitch - tall))).reshape(targets, ORDER * pitch)
     top = table.astype(jnp.bfloat16)
     rest = (table - top.astype(np.float32)).astype(jnp.bfloat16)
     table = jnp.asarray(np.concatenate([top, rest], 0))
-    early = stations <= s_
-    groups = stations if early else s_
-    chosen = station_of if early else jnp.arange(s_, dtype=jnp.int32)
     modes = jnp.asarray(radial_modes(r_)[:WALL_SPAN].astype(np.float32))
-    pick = (wall_index[:, None] == jnp.arange(WALL_SPAN)[None, :]).astype(jnp.float32)
+    pick = (near_walls[:, None] == jnp.arange(WALL_SPAN)[None, :]).astype(jnp.float32)
     values = jnp.dot(pick, modes, precision=PRECISE)
     rates = jnp.asarray(radial_rates(r_))[None, :]
     tall_rows = ORDER * groups
 
-    def kernel(s_in, near, far, tab, station, rate, value, base, out, parts, high, low, terms, old, new):
+    def kernel(s_in, tab, station, rate, value, base, out, parts, high, low, terms, old, new):
         k = pl.program_id(0)
 
         @pl.when(k == 0)
         def _():
-            pick = (lax.broadcasted_iota(jnp.int32, (groups, s_), 0) == station[...]).astype(jnp.bfloat16)
+            pick = (lax.broadcasted_iota(jnp.int32, (groups, targets), 0) == station[...]).astype(jnp.bfloat16)
             whole = jnp.dot(jnp.concatenate([pick, pick], axis=1), tab[...], preferred_element_type=jnp.float32)
             for j in range(ORDER):
                 top, rest = split(whole[:, j * pitch : j * pitch + rows])
                 parts[j * groups : (j + 1) * groups] = top
                 parts[tall_rows + j * groups : tall_rows + (j + 1) * groups] = rest
 
-        for i in range(TILE):
-            own = s_in[i]
-            before, at_low, at_high, after = slab_parts(own, near[i], far[i], s_)
-            slab = jnp.concatenate(
-                [before, own[:TILE] + at_low]
-                + ([own[TILE : s_ - TILE]] if s_ > 2 * TILE else [])
-                + [own[s_ - TILE : s_] + at_high, after],
-                0,
-            )
-            top, rest = split(slab)
-            high[:, i * r_ : (i + 1) * r_] = top
-            low[:, i * r_ : (i + 1) * r_] = rest
-        one = jnp.dot(parts[...], high[...], preferred_element_type=jnp.float32)
-        two = jnp.dot(parts[:tall_rows], low[...], preferred_element_type=jnp.float32)
-        terms[k] = one[:tall_rows] + one[tall_rows:] + two
+        for c in range(group):
+            for i in range(TILE):
+                slab = s_in[c * TILE + i]
+                if rows > tall:
+                    slab = jnp.concatenate([slab, jnp.zeros((rows - tall, r_), jnp.float32)], 0)
+                top, rest = split(slab)
+                high[c, :, i * r_ : (i + 1) * r_] = top
+                low[c, :, i * r_ : (i + 1) * r_] = rest
+            one = jnp.dot(parts[...], high[c], preferred_element_type=jnp.float32)
+            two = jnp.dot(parts[:tall_rows], low[c], preferred_element_type=jnp.float32)
+            terms[k * group + c] = one[:tall_rows] + one[tall_rows:] + two
 
         @pl.when(k == steps - 1)
         def _():
@@ -460,7 +474,7 @@
                     old[c * TILE + i + 1] = terms[c, first : first + groups, i * r_ : (i + 1) * r_]
                 return 0
 
-            lax.fori_loop(0, steps, start, 0)
+            lax.fori_loop(0, chunks, start, 0)
             source, target = old, new
             for j in range(ORDER - 2, -1, -1):
 
@@ -475,14 +489,14 @@
                         )
                     return 0
 
-                lax.fori_loop(0, steps, level, 0)
+                lax.fori_loop(0, chunks, level, 0)
                 source, target = target, source
             ones = jnp.ones((2 * r_, NA), jnp.bfloat16)
 
             def gather(c, total):
                 for i in range(TILE):
                     t = c * TILE + i
-                    product = source[t + LEAD + 1] * value[pl.ds(t, 1), :]
+                    product = source[t + 1] * value[pl.ds(t, 1), :]
                     top, rest = split(product)
                     sums = jnp.dot(
                         jnp.concatenate([top, rest], axis=1), ones, preferred_element_type=jnp.float32
@@ -490,37 +504,32 @@
                     total = total + sums * base[pl.ds(t, 1), :]
                 return total
 
-            out[...] = lax.fori_loop(0, t_ // TILE, gather, jnp.zeros((groups, NA), jnp.float32))
+            out[...] = lax.fori_loop(0, chunks, gather, jnp.zeros((groups, NA), jnp.float32))
 
     tile = pl.pallas_call(
         kernel,
         grid=(steps,),
         in_specs=[
-            pl.BlockSpec((TILE, tall, r_), lambda k: (k, 0, 0)),
-            pl.BlockSpec((TILE, TILE, r_), lambda k: (k, 0, 0)),
-            pl.BlockSpec((TILE, TILE, r_), lambda k: (k, 0, 0)),
-            pl.BlockSpec((2 * s_, ORDER * pitch), lambda k: (0, 0)),
-            pl.BlockSpec((1, s_), lambda k: (0, 0)),
+            pl.BlockSpec((group * TILE, tall, r_), lambda k: (k, 0, 0)),
+            pl.BlockSpec((2 * targets, ORDER * pitch), lambda k: (0, 0)),
+            pl.BlockSpec((1, targets), lambda k: (0, 0)),
             pl.BlockSpec((1, r_), lambda k: (0, 0)),
-            pl.BlockSpec((t_, r_), lambda k: (0, 0)),
-            pl.BlockSpec((t_, NA), lambda k: (0, 0)),
+            pl.BlockSpec((wide, r_), lambda k: (0, 0)),
+            pl.BlockSpec((wide, NA), lambda k: (0, 0)),
         ],
         out_specs=pl.BlockSpec((groups, NA), lambda k: (0, 0)),
         out_shape=jax.ShapeDtypeStruct((groups, NA), jnp.float32),
         scratch_shapes=[
             pltpu.VMEM((2 * tall_rows, rows), jnp.bfloat16),
-            pltpu.VMEM((rows, TILE * r_), jnp.bfloat16),
-            pltpu.VMEM((rows, TILE * r_), jnp.bfloat16),
-            pltpu.VMEM((steps, tall_rows, TILE * r_), jnp.float32),
+            pltpu.VMEM((group, rows, TILE * r_), jnp.bfloat16),
+            pltpu.VMEM((group, rows, TILE * r_), jnp.bfloat16),
+            pltpu.VMEM((chunks, tall_rows, TILE * r_), jnp.float32),
             pltpu.VMEM((wide + 2, groups, r_), jnp.float32),
             pltpu.VMEM((wide + 2, groups, r_), jnp.float32),
         ],
         compiler_params=pltpu.CompilerParams(vmem_limit_bytes=56 << 20),
         name="wall",
-    )(s_ext, pack_l, pack_r, table, chosen[None, :], rates, values, basis)
-    if not early:
-        select = (station_of[:, None] == jnp.arange(stations)[None, :]).astype(jnp.float32)
-        tile = jnp.dot(select.T, tile, precision=PRECISE)
+    )(s_ext, table, chosen[None, :], rates, values, near_basis)
     return tile
 
 
@@ -552,40 +561,61 @@
     return lax.ppermute(x, ("span", "plane"), pairs)
 
 
-def exchange(s_ext, zr, zl, spans, planes, span_cells, theta_cells):
+def turn_exchange(s_ext, zr, zl, wall_index, spans, planes):
+    theta_cells = wall_index.shape[0]
+    tall = s_ext.shape[1]
     edge = ORDER + 1
+    wide = s_ext.shape[0]
     first = LEAD - 1
     last = LEAD + theta_cells - ORDER
     after = LEAD - ORDER
     before = LEAD + theta_cells - 1
 
-    def planes_of(z, step):
-        mid = send(z, spans, planes, step, 0)
-        low = send(z[last : last + edge], spans, planes, step, 1)
-        high = send(z[first : first + edge], spans, planes, step, -1)
-        total = mid.shape[0]
-        low = jnp.pad(low, ((after, total - after - edge), (0, 0), (0, 0)))
-        high = jnp.pad(high, ((before, total - before - edge), (0, 0), (0, 0)))
-        return mid + low + high
-
-    low = send(s_ext[last : last + edge], spans, planes, 0, 1)
-    high = send(s_ext[first : first + edge], spans, planes, 0, -1)
-    from_left = planes_of(zr, 1)
-    from_right = planes_of(zl, -1)
-    hop = 1
-    while hop < spans and np.any(hop_table(hop * span_cells)):
-        table = hop_table(hop * span_cells)
+    def packed(at, walls):
+        free = jnp.pad(walls.astype(jnp.float32), (0, zr.shape[2] - ORDER))
+        own = zr[at : at + edge]
+        own = jnp.where(jnp.arange(TILE)[None, :, None] == 1, free[None, None, :], own)
+        return jnp.concatenate([s_ext[at : at + edge], own, zl[at : at + edge]], axis=1)
+
+    low = send(packed(last, wall_index[-ORDER:]), spans, planes, 0, 1)
+    high = send(packed(first, wall_index[:ORDER]), spans, planes, 0, -1)
+
+    def unpacked():
+        rows = jnp.arange(TILE)[None, :, None] != 1
+        whole = []
+        for mid, start in ((zr, tall), (zl, tall + TILE)):
+            sides = []
+            for piece, at in ((low, after), (high, before)):
+                piece = piece[:, start : start + TILE]
+                if start == tall:
+                    piece = jnp.where(rows, piece, 0.0)
+                sides.append(jnp.pad(piece, ((at, wide - at - edge), (0, 0), (0, 0))))
+            whole.append(mid + sides[0] + sides[1])
+        walls = [piece[0, tall + 1, :ORDER].astype(wall_index.dtype) for piece in (low, high)]
+        none = jnp.full((wide,), -1, wall_index.dtype)
+        walls = jnp.concatenate(
+            [none[:after], walls[0], wall_index, walls[1], none[LEAD + theta_cells + ORDER :]], 0
+        )
+        return whole[0], whole[1], walls
+
+    return low, high, unpacked
+
+
+def span_exchange(zr, zl, spans, planes, span_cells):
+    from_left = [send(zr, spans, planes, 1, 0)]
+    from_right = [send(zl, spans, planes, -1, 0)]
+    tables = []
+    while len(from_left) < spans and np.any(hop_table(len(from_left) * span_cells)):
+        table = hop_table(len(from_left) * span_cells)
         left_table = np.zeros((TILE, TILE), np.float32)
         left_table[: TILE - ORDER - 1 : -1, [0, 7, 6, 5, 4, 3]] = table
         right_table = np.zeros((TILE, TILE), np.float32)
         right_table[:ORDER, [7, 0, 1, 2, 3, 4]] = table
-        far_left = planes_of(zr, hop + 1)
-        far_right = planes_of(zl, -hop - 1)
-        from_left = from_left + jnp.einsum("bd,adr->abr", left_table, far_left, precision=PRECISE)
-        from_right = from_right + jnp.einsum("bd,adr->abr", right_table, far_right, precision=PRECISE)
-        hop += 1
-    s_ext = s_ext.at[after : after + edge].add(low).at[before : before + edge].add(high)
-    return s_ext, from_left, from_right
+        tables.append((left_table, right_table))
+        hop = len(from_left) + 1
+        from_left.append(send(zr, spans, planes, hop, 0))
+        from_right.append(send(zl, spans, planes, -hop, 0))
+    return from_left, from_right, tables
 
 
 def share(rows, spans, planes):
@@ -603,13 +633,30 @@
     _, span_cells, theta_cells, _ = velocity.shape
     total_theta = theta_cells * planes
     stations = ST_DEV * spans
-    basis = azimuth_basis(lax.axis_index("plane") * theta_cells, theta_cells, total_theta)
-    s_ext, zr, zl = source_call(velocity)
+    wide = theta_cells + 2 * TILE
+    hops = wall_hops(span_cells)
+    near_basis = azimuth_basis(lax.axis_index("plane") * theta_cells - LEAD, wide, total_theta)
+    basis = near_basis[LEAD : LEAD + theta_cells]
+    s_own, zr, zl = source_call(velocity)
+    station_of, wall_index, s_own = lax.optimization_barrier((station_of, wall_index, s_own))
+    low, high, unpacked = turn_exchange(s_own, zr, zl, wall_index, spans, planes)
+    sides = [send(station_of, spans, planes, -h, 0) if h else station_of for h in range(-hops, hops + 1)]
     tiles = bins_call(wall_history, phase_bin, station_of, basis, stations)
-    s_ext, pack_l, pack_r = exchange(s_ext, zr, zl, spans, planes, span_cells, theta_cells)
-    wall = wall_call(s_ext, pack_l, pack_r, station_of, wall_index, basis, stations)
+    zr_wide, zl_wide, near_walls = unpacked()
+    zr_wide, zl_wide, near_walls, sides, tiles = lax.optimization_barrier((zr_wide, zl_wide, near_walls, sides, tiles))
+    from_left, from_right, tables = span_exchange(zr_wide, zl_wide, spans, planes, span_cells)
+    near_stations = jnp.concatenate(sides, 0)
+    wall = wall_call(s_own, near_stations, near_walls, near_basis, stations)
     newest = (jnp.arange(NBIN) == phase_bin[-1]).astype(jnp.float32)
     tiles = tiles + newest[None, :, None] * wall[:, None, :]
+    from_left, from_right, tiles, s_own = lax.optimization_barrier((from_left, from_right, tiles, s_own))
+    tall = span_cells + TILE
+    s_ext = s_own.at[LEAD - ORDER : LEAD + 1].add(low[:, :tall])
+    s_ext = s_ext.at[LEAD + theta_cells - 1 : LEAD + theta_cells + ORDER].add(high[:, :tall])
+    pack_l, pack_r = from_left[0], from_right[0]
+    for far_left, far_right, (left_table, right_table) in zip(from_left[1:], from_right[1:], tables):
+        pack_l = pack_l + jnp.einsum("bd,adr->abr", left_table, far_left, precision=PRECISE)
+        pack_r = pack_r + jnp.einsum("bd,adr->abr", right_table, far_right, precision=PRECISE)
     each = stations // (spans * planes)
     parts = lax.all_to_all(tiles, ("span", "plane"), split_axis=0, concat_axis=0, tiled=True)
     corrected, pressure = project_call(s_ext, pack_l, pack_r, velocity)

time: 159 us -> 140 us (0.88)
  Pallas kernels: 110 us -> 95.6 us
  waiting for transfers between devices: 11.5 us -> 7.65 us
  starting transfers between devices: 21.5 us -> 18.3 us
  other arithmetic: 9.23 us -> 11 us
    pallas_call x2, Pallas kernels: 73.1 us -> 61 us  [the longest x1 45.1 us: project_call(): pl.pallas_call(body, grid=(steps + 1,), in_specs=[pl.BlockSpec((TILE, s_...]
    ppermute x11 -> x9, waiting for transfers between devices: 11.5 us -> 7.65 us  [send(): return lax.ppermute(x, ('span', 'plane'), pairs)]
    all_to_all x1, starting transfers between devices: 7.11 us -> 3.69 us  [local(): lax.all_to_all(tiles, ('span', 'plane'), split_axis=0, concat_axis=0, til...]
    pallas_call x1, Pallas kernels: 25.6 us -> 22.9 us  [source_call(): pl.pallas_call(body, grid=(wide // TILE,), in_specs=[part(0), part(1), pa...]
    scatter-add x1 -> x2, other arithmetic: 1.81 us -> 3.85 us  [the longest x1 1.93 us: local(): s_ext.at[LEAD + theta_cells - 1:LEAD + theta_cells + ORDER]]
    slice x1 -> x2, other arithmetic: 1.96 us -> 0.15 us  [unpacked(): piece = piece[:, start:start + TILE]]
    add x2, other arithmetic: 1.71 us -> 0.09 us  [the longest x1 0.08 us: unpacked(): whole.append(mid + sides[0] + sides[1])]
    concatenate x0 -> x3, other arithmetic: none -> 1.61 us  [the longest x2 1.6 us: packed(): return jnp.concatenate([s_ext[at:at + edge], own, zl[at:at + edge]], axis=1)]
  transfers between devices with their start and end apart: 12 -> 10, of which waited for: 6 -> 4; matrix products, arithmetic and copies ran while one was open for 4% -> 9% of each run, Pallas kernels for 40% -> 52%
where the time goes in v3:
time: 140 us; the launch traced here: 139 us
  Pallas kernels  95.6 us (68%)
  starting transfers between devices  18.3 us (13%)
  other arithmetic  11 us (8%)
  waiting for transfers between devices  7.65 us (5%)
  local copies, waits for them, and re-layouts  3.86 us (3%)
    pallas_call x1, Pallas kernels, project_call(): pl.pallas_call(body, grid=(steps + 1,), in_specs=[pl.BlockSpec((TILE, s_...  45.1 us
    pallas_call x1, Pallas kernels, source_call(): pl.pallas_call(body, grid=(wide // TILE,), in_specs=[part(0), part(1), pa...  22.9 us
    pallas_call x1, Pallas kernels, wall_part(): pl.pallas_call(kernel, grid=(steps,), in_specs=[pl.BlockSpec((group * TIL...  15.9 us
    ppermute x9, starting transfers between devices, send(): return lax.ppermute(x, ('span', 'plane'), pairs)  14.7 us
    pallas_call x1, Pallas kernels, bins_call(): pl.pallas_call(kernel, grid_spec=pltpu.PrefetchScalarGridSpec(num_scalar_...  11.6 us
    ppermute x9, waiting for transfers between devices, send(): return lax.ppermute(x, ('span', 'plane'), pairs)  7.65 us
    all_to_all x1, starting transfers between devices, local(): lax.all_to_all(tiles, ('span', 'plane'), split_axis=0, concat_axis=0, til...  3.69 us
  transfers between devices with their start and end apart: 10, of which 4 were waited for; matrix products, arithmetic and copies ran while one was open for 9% of the time, Pallas kernels for 52%

profile of v3, /device:TPU:0, one launch (start us, length us, event | category | flops | bytes accessed | tf_op | source)
XLA Modules:
  0.0 138.6 jit_solution(10884170705715144660)
XLA Ops:
  0.6 0.0 copy-start.1
  0.6 0.9 copy-done.1
  1.6 0.7 copy-done.2
  2.3 22.9 %source.1 = (f32[144,136,128]{2,1,0:T(8,128)S(1)}, f32[144,8,128]{2,1,0:T(8,128)S(1)}, f32[144,8,128]{2,1,0:T(8,128)S(1)}) custom-call(f32[3,128,128,128]{3,2,1,0:T(8,128)} %v.1, f32[3,128,128,128]{3,2,1,0:T(8,128)} %v.1, f32[3,128,128,128]{3,2,1,0:T(8,128)} %v.1, bf16[32,128]{1,0:T(8,128)(2,1)S(1)} %copy-done.2, bf16[768,128]{1,0:T(8,128)(2,1)S(1)} %copy-done.1), custom_call_target="tpu_custom_call" | custom-call | tf_op jit(solution)/shard_map/source/pallas_call | solution.py:185
  25.2 0.0 copy-start
  25.2 0.0 copy-done.3
  25.2 3.0 %collective-permute-start.2 = (s32[128]{0:T(128)S(1)}, s32[128]{0:T(128)S(1)}, u32[]{:S(2)}, u32[]{:S(2)}) collective-permute-start(s32[128]{0:T(128)S(1)} %copy-done.3), channel_id=1, source_target_pairs={{0,4},{1,5},{2,6},{3,7},{4,8},{5,9},{6,10},{7,11},{8,12},{9,13},{1... | collective-permute-start | bytes 1544 | tf_op jit(solution)/shard_map/ppermute | solution.py:561
  28.2 3.1 %collective-permute-start.3 = (s32[128]{0:T(128)S(1)}, s32[128]{0:T(128)S(1)}, u32[]{:S(2)}, u32[]{:S(2)}) collective-permute-start(s32[128]{0:T(128)S(1)} %copy-done.3), channel_id=1, source_target_pairs={{0,28},{1,29},{2,30},{3,31},{4,0},{5,1},{6,2},{7,3},{8,4},{9,5},{1... | collective-permute-start | bytes 1544 | tf_op jit(solution)/shard_map/ppermute | solution.py:561
  31.3 0.0 copy-done.10
  31.3 0.1 slice_convert_fusion.3
  31.4 0.0 copy-done
  31.4 0.1 fusion.35
  31.5 0.1 slice_select_fusion.3
  31.6 0.8 pad_maximum_fusion
  32.4 0.0 collective-permute-start
  32.4 0.8 pad_maximum_fusion.1
  33.2 1.7 %collective-permute-start.1 = (f32[6,152,128]{2,1,0:T(8,128)}, f32[6,152,128]{2,1,0:T(8,128)S(1)}, u32[]{:S(2)}, u32[]{:S(2)}) collective-permute-start(f32[6,152,128]{2,1,0:T(8,128)} %pad_maximum_fusion.1), channel_id=1, source_target_pairs={{0,3},{1,0},{2,1},{3,2},{4,7},{5,4},{6,5},{7,6},{8,11},{9,8},{10,9... | collective-permute-start | bytes 1400840 | tf_op jit(solution)/shard_map/ppermute | solution.py:561
  34.9 0.4 cosine_select_fusion.base
  35.3 0.0 copy-start.5
  35.3 0.0 copy-done.4
  35.3 0.6 slice.117
  35.9 11.6 %bins.2 = f32[2048,128]{1,0:T(8,128)S(1)} custom-call(s32[256]{0:T(256)S(1)} %copy-done.4, f32[255,128,128]{2,1,0:T(8,128)} %x.13, s32[1,128]{1,0:T(1,128)S(1)} %bitcast.13, f32[128,128]{1,0:T(8,128)S(1)} %slice.128.base), custom_call_target="tpu_custom_call" | custom-call | tf_op jit(solution)/shard_map/bins/pallas_call | solution.py:255
  47.6 0.7 compare_convert_fusion
  48.2 0.0 collective-permute-done
  48.2 0.0 copy-start.8
  48.3 0.1 fusion.37
  48.3 0.0 collective-permute-done.1
  48.3 0.1 fusion.38
  48.4 0.6 copy-done.8
  49.0 0.2 copy-done.9
  49.2 0.1 pad_add_fusion
  49.3 0.0 copy-done.5
  49.3 0.7 fusion.29
  50.0 0.7 fusion.28
  50.7 0.1 concatenate.18
  50.7 0.0 collective-permute-done.2
  50.7 0.0 collective-permute-done.3
  50.8 0.6 collective-permute-start.4
  51.4 4.2 %collective-permute-start.5 = (f32[144,8,128]{2,1,0:T(8,128)S(1)}, f32[144,8,128]{2,1,0:T(8,128)S(1)}, u32[]{:S(2)}, u32[]{:S(2)}) collective-permute-start(f32[144,8,128]{2,1,0:T(8,128)S(1)} %get-tuple-element.55), channel_id=1, source_target_pairs={{0,28},{1,29},{2,30},{3,31},{4,0},{5,1},{6,2},{7,3},{8,4},{9,5},{1... | collective-permute-start | bytes 1769480 | tf_op jit(solution)/shard_map/ppermute | solution.py:561
  55.5 0.5 broadcast_in_dim.155.station
  56.1 0.0 copy-done.11
  56.1 0.9 fusion.5.value
  56.9 15.9 %wall.1 = f32[32,128]{1,0:T(8,128)} custom-call(f32[144,136,128]{2,1,0:T(8,128)} %copy-done, bf16[768,1280]{1,0:T(8,128)(2,1)} %constant.168.clone.tab, s32[1,384]{1,0:T(1,128)} %broadcast_in_dim.155.station, f32[1,128]{1,0:T(1,128)} %constant.185.rate, f32[144,128]{1,0:T(8,128)} %fusion.5.value, f32[144,128]{1,0:T(8,128)} %copy-done.5), custom_call_target="tpu_custom_call" | custom-call | tf_op jit(solution)/shard_map/wall/pallas_call | solution.py:509
  72.8 1.9 %multiply_add_fusion = f32[32,64,128]{2,1,0:T(8,128)} fusion(f32[32,64,128]{2,1,0:T(8,128)S(1)} %bitcast.12, f32[32,128]{1,0:T(8,128)} %wall.1, f32[64]{0:T(128)S(1)} %compare_convert_fusion), kind=kLoop, calls=%fused_computation | loop fusion | flops 524288 | bytes 2113792 | tf_op jit(solution)/shard_map/add | solution.py:651
  74.7 1.9 %collective-permute-done.4.near = f32[144,8,128]{2,1,0:T(8,128)S(1)} collective-permute-done((f32[144,8,128]{2,1,0:T(8,128)S(1)}, f32[144,8,128]{2,1,0:T(8,128)S(1)}, u32[]{:S(2)}, u32[]{:S(2)}) %collective-permute-start.4) | collective-permute-done | bytes 589856 | tf_op jit(solution)/shard_map/ppermute | solution.py:561
  76.6 2.2 %collective-permute-done.5.far = f32[144,8,128]{2,1,0:T(8,128)S(1)} collective-permute-done((f32[144,8,128]{2,1,0:T(8,128)S(1)}, f32[144,8,128]{2,1,0:T(8,128)S(1)}, u32[]{:S(2)}, u32[]{:S(2)}) %collective-permute-start.5) | collective-permute-done | bytes 589856 | tf_op jit(solution)/shard_map/ppermute | solution.py:561
  78.8 3.7 %all-to-all-start = ((f32[32,64,128]{2,1,0:T(8,128)}), f32[32,64,128]{2,1,0:T(8,128)S(1)}, u32[]{:S(2)}, u32[]{:S(2)}) async-start(f32[32,64,128]{2,1,0:T(8,128)} %multiply_add_fusion), calls=%async_computation | async-start | bytes 2097152 | tf_op jit(solution)/shard_map/all_to_all | solution.py:661
  82.6 1.9 %fusion.1 = f32[144,136,128]{2,1,0:T(8,128)} fusion(f32[144,136,128]{2,1,0:T(8,128)} %copy-done, f32[6,152,128]{2,1,0:T(8,128)} %copy-done.8), kind=kLoop, calls=%fused_computation.8 | loop fusion | flops 104448 | bytes 1253376 | tf_op jit(solution)/shard_map/scatter-add | solution.py:654
  84.6 1.9 %fusion.s_in = f32[144,136,128]{2,1,0:T(8,128)} fusion(f32[144,136,128]{2,1,0:T(8,128)} %fusion.1, f32[6,152,128]{2,1,0:T(8,128)} %copy-done.9), kind=kLoop, calls=%fused_computation.6 | loop fusion | flops 104448 | bytes 1253376 | tf_op jit(solution)/shard_map/scatter-add | solution.py:655
  86.5 0.0 copy-done.6
  86.5 0.0 copy-done.7
  86.5 45.1 %project.1 = (f32[3,128,128,128]{3,2,1,0:T(8,128)}, f32[128,128,128]{2,1,0:T(8,128)}) custom-call(f32[144,136,128]{2,1,0:T(8,128)} %fusion.s_in, f32[144,8,128]{2,1,0:T(8,128)} %copy-done.6, f32[144,8,128]{2,1,0:T(8,128)} %copy-done.7, f32[3,128,128,128]{3,2,1,0:T(8,128)} %v.1, bf16[272,160]{1,0:T(8,128)(2,1)} %constant.171.clone.tab, ...), custom_call_target="tpu_custom_call" | custom-call | tf_op jit(solution)/shard_map/project/pallas_call | solution.py:378
  131.6 0.0 all-to-all-done
  131.6 0.1 reduce_sum.9
  131.7 0.3 fusion.10
  132.0 0.1 reshape.219
  132.1 1.6 %collective-permute-start.6 = (f32[1,8192]{1,0:T(1,128)S(1)}, f32[1,8192]{1,0:T(1,128)S(1)}, u32[]{:S(2)}, u32[]{:S(2)}) collective-permute-start(f32[1,8192]{1,0:T(1,128)S(1)} %reshape.219), channel_id=1, source_target_pairs={{0,3},{1,0},{2,1},{3,2},{4,7},{5,4},{6,5},{7,6},{8,11},{9,8},{10,9... | collective-permute-start | bytes 98312 | tf_op jit(solution)/shard_map/ppermute | solution.py:561
  133.7 0.4 collective-permute-start.7
  134.1 0.1 collective-permute-start.8
  134.2 0.1 broadcast_in_dim.169
  134.3 1.0 collective-permute-done.6
  135.3 2.5 %collective-permute-done.7 = f32[1,8192]{1,0:T(1,128)S(1)} collective-permute-done((f32[1,8192]{1,0:T(1,128)S(1)}, f32[1,8192]{1,0:T(1,128)S(1)}, u32[]{:S(2)}, u32[]{:S(2)}) %collective-permute-start.7) | collective-permute-done | bytes 32800 | tf_op jit(solution)/shard_map/ppermute | solution.py:561
  137.8 0.0 collective-permute-done.8
  137.8 0.8 select_select_fusion
  (24 shorter events, 0.1 us)
Async XLA Ops:
  0.6 0.9 copy-start.1
  1.6 0.7 copy-start.2
  2.3 23.0 %copy-start.3 = (s32[128]{0:T(128)S(1)}, s32[128]{0:T(128)}, u32[]{:S(2)}) copy-start(s32[128]{0:T(128)} %param.20) | copy-start | bytes 1540
  2.3 29.1 %copy-start.10 = (s32[128]{0:T(128)S(1)}, s32[128]{0:T(128)}, u32[]{:S(2)}) copy-start(s32[128]{0:T(128)} %param.21) | copy-start | bytes 1540
  2.3 33.1 %copy-start.4 = (s32[256]{0:T(256)S(1)}, s32[256]{0:T(256)}, u32[]{:S(2)}) copy-start(s32[256]{0:T(256)} %bins.3) | copy-start | bytes 3076
  25.2 6.2 %copy-start = (f32[144,136,128]{2,1,0:T(8,128)}, f32[144,136,128]{2,1,0:T(8,128)S(1)}, u32[]{:S(2)}) copy-start(f32[144,136,128]{2,1,0:T(8,128)S(1)} %get-tuple-element.61.s_in) | copy-start | bytes 30081028
  25.2 25.5 %collective-permute-start.2 = (s32[128]{0:T(128)S(1)}, s32[128]{0:T(128)S(1)}, u32[]{:S(2)}, u32[]{:S(2)}) collective-permute-start(s32[128]{0:T(128)S(1)} %copy-done.3), channel_id=1, source_target_pairs={{0,4},{1,5},{2,6},{3,7},{4,8},{5,9},{6,10},{7,11},{8,12},{9,13},{1... | collective-permute-start | bytes 1544 | tf_op jit(solution)/shard_map/ppermute | solution.py:561
  28.2 22.5 %collective-permute-start.3 = (s32[128]{0:T(128)S(1)}, s32[128]{0:T(128)S(1)}, u32[]{:S(2)}, u32[]{:S(2)}) collective-permute-start(s32[128]{0:T(128)S(1)} %copy-done.3), channel_id=1, source_target_pairs={{0,28},{1,29},{2,30},{3,31},{4,0},{5,1},{6,2},{7,3},{8,4},{9,5},{1... | collective-permute-start | bytes 1544 | tf_op jit(solution)/shard_map/ppermute | solution.py:561
  32.4 15.9 %collective-permute-start = (f32[6,152,128]{2,1,0:T(8,128)}, f32[6,152,128]{2,1,0:T(8,128)S(1)}, u32[]{:S(2)}, u32[]{:S(2)}) collective-permute-start(f32[6,152,128]{2,1,0:T(8,128)} %pad_maximum_fusion), channel_id=1, source_target_pairs={{0,1},{1,2},{2,3},{3,0},{4,5},{5,6},{6,7},{7,4},{8,9},{9,10},{10,1... | collective-permute-start | bytes 1400840 | tf_op jit(solution)/shard_map/ppermute | solution.py:561
  33.2 15.2 %collective-permute-start.1 = (f32[6,152,128]{2,1,0:T(8,128)}, f32[6,152,128]{2,1,0:T(8,128)S(1)}, u32[]{:S(2)}, u32[]{:S(2)}) collective-permute-start(f32[6,152,128]{2,1,0:T(8,128)} %pad_maximum_fusion.1), channel_id=1, source_target_pairs={{0,3},{1,0},{2,1},{3,2},{4,7},{5,4},{6,5},{7,6},{8,11},{9,8},{10,9... | collective-permute-start | bytes 1400840 | tf_op jit(solution)/shard_map/ppermute | solution.py:561
  35.3 14.0 %copy-start.5 = (f32[144,128]{1,0:T(8,128)}, f32[144,128]{1,0:T(8,128)S(1)}, u32[]{:S(2)}) copy-start(f32[144,128]{1,0:T(8,128)S(1)} %cosine_select_fusion.base) | copy-start | bytes 221188
  35.9 20.1 %copy-start.11 = (f32[8,128]{1,0:T(8,128)S(1)}, f32[8,128]{1,0:T(8,128)}, u32[]{:S(2)}) copy-start(f32[8,128]{1,0:T(8,128)} %constant.169.clone) | copy-start | bytes 12292
  48.2 0.8 copy-start.8
  48.3 0.8 copy-start.9
  50.8 25.9 %collective-permute-start.4 = (f32[144,8,128]{2,1,0:T(8,128)S(1)}, f32[144,8,128]{2,1,0:T(8,128)S(1)}, u32[]{:S(2)}, u32[]{:S(2)}) collective-permute-start(f32[144,8,128]{2,1,0:T(8,128)S(1)} %get-tuple-element.54), channel_id=1, source_target_pairs={{0,4},{1,5},{2,6},{3,7},{4,8},{5,9},{6,10},{7,11},{8,12},{9,13},{1... | collective-permute-start | bytes 1769480 | tf_op jit(solution)/shard_map/ppermute | solution.py:561
  51.4 27.5 %collective-permute-start.5 = (f32[144,8,128]{2,1,0:T(8,128)S(1)}, f32[144,8,128]{2,1,0:T(8,128)S(1)}, u32[]{:S(2)}, u32[]{:S(2)}) collective-permute-start(f32[144,8,128]{2,1,0:T(8,128)S(1)} %get-tuple-element.55), channel_id=1, source_target_pairs={{0,28},{1,29},{2,30},{3,31},{4,0},{5,1},{6,2},{7,3},{8,4},{9,5},{1... | collective-permute-start | bytes 1769480 | tf_op jit(solution)/shard_map/ppermute | solution.py:561
  76.6 9.8 %copy-start.6 = (f32[144,8,128]{2,1,0:T(8,128)}, f32[144,8,128]{2,1,0:T(8,128)S(1)}, u32[]{:S(2)}) copy-start(f32[144,8,128]{2,1,0:T(8,128)S(1)} %collective-permute-done.4.near) | copy-start | bytes 1769476
  78.8 7.6 %copy-start.7 = (f32[144,8,128]{2,1,0:T(8,128)}, f32[144,8,128]{2,1,0:T(8,128)S(1)}, u32[]{:S(2)}) copy-start(f32[144,8,128]{2,1,0:T(8,128)S(1)} %collective-permute-done.5.far) | copy-start | bytes 1769476
  78.8 52.7 %all-to-all-start = ((f32[32,64,128]{2,1,0:T(8,128)}), f32[32,64,128]{2,1,0:T(8,128)S(1)}, u32[]{:S(2)}, u32[]{:S(2)}) async-start(f32[32,64,128]{2,1,0:T(8,128)} %multiply_add_fusion), calls=%async_computation | async-start | bytes 2097152 | tf_op jit(solution)/shard_map/all_to_all | solution.py:661
  132.1 3.2 %collective-permute-start.6 = (f32[1,8192]{1,0:T(1,128)S(1)}, f32[1,8192]{1,0:T(1,128)S(1)}, u32[]{:S(2)}, u32[]{:S(2)}) collective-permute-start(f32[1,8192]{1,0:T(1,128)S(1)} %reshape.219), channel_id=1, source_target_pairs={{0,3},{1,0},{2,1},{3,2},{4,7},{5,4},{6,5},{7,6},{8,11},{9,8},{10,9... | collective-permute-start | bytes 98312 | tf_op jit(solution)/shard_map/ppermute | solution.py:561
  133.7 4.1 %collective-permute-start.7 = (f32[1,8192]{1,0:T(1,128)S(1)}, f32[1,8192]{1,0:T(1,128)S(1)}, u32[]{:S(2)}, u32[]{:S(2)}) collective-permute-start(f32[1,8192]{1,0:T(1,128)S(1)} %reshape.219), channel_id=1, source_target_pairs={{0,2},{1,3},{2,0},{3,1},{4,6},{5,7},{6,4},{7,5},{8,10},{9,11},{10,... | collective-permute-start | bytes 98312 | tf_op jit(solution)/shard_map/ppermute | solution.py:561
  134.1 3.7 %collective-permute-start.8 = (f32[1,8192]{1,0:T(1,128)S(1)}, f32[1,8192]{1,0:T(1,128)S(1)}, u32[]{:S(2)}, u32[]{:S(2)}) collective-permute-start(f32[1,8192]{1,0:T(1,128)S(1)} %reshape.219), channel_id=1, source_target_pairs={{0,1},{1,2},{2,3},{3,0},{4,5},{5,6},{6,7},{7,4},{8,9},{9,10},{10,1... | collective-permute-start | bytes 98312 | tf_op jit(solution)/shard_map/ppermute | solution.py:561

commit v4 on v3

--- a/solution.py
+++ b/solution.py
@@ -217,7 +217,7 @@
 def bins_call(wall_history, phase_bin, station_of, basis, stations):
     h, s_, t_ = wall_history.shape
     step = max(d for d in range(1, 52) if h % d == 0)
-    pair = 2
+    pair = 4
     def kernel(bins, x, station, base, out, acc):
         c = pl.program_id(0)
 
@@ -494,14 +494,12 @@
             ones = jnp.ones((2 * r_, NA), jnp.bfloat16)
 
             def gather(c, total):
-                for i in range(TILE):
-                    t = c * TILE + i
-                    product = source[t + 1] * value[pl.ds(t, 1), :]
-                    top, rest = split(product)
-                    sums = jnp.dot(
-                        jnp.concatenate([top, rest], axis=1), ones, preferred_element_type=jnp.float32
-                    )
-                    total = total + sums * base[pl.ds(t, 1), :]
+                at = [c * TILE + i for i in range(TILE)]
+                product = jnp.concatenate([source[t + 1] * value[pl.ds(t, 1), :] for t in at], axis=0)
+                top, rest = split(product)
+                sums = jnp.dot(jnp.concatenate([top, rest], axis=1), ones, preferred_element_type=jnp.float32)
+                for i, t in enumerate(at):
+                    total = total + sums[i * groups : (i + 1) * groups] * base[pl.ds(t, 1), :]
                 return total
 
             out[...] = lax.fori_loop(0, chunks, gather, jnp.zeros((groups, NA), jnp.float32))

time: 140 us -> 140 us (level)
  no operation moved by 1% of the time
where the time goes in v4:
time: 140 us; the launch traced here: 139 us
  Pallas kernels  95.2 us (68%)
  starting transfers between devices  18.3 us (13%)
  other arithmetic  11 us (8%)
  waiting for transfers between devices  8.14 us (6%)
  local copies, waits for them, and re-layouts  3.86 us (3%)
    pallas_call x1, Pallas kernels, project_call(): pl.pallas_call(body, grid=(steps + 1,), in_specs=[pl.BlockSpec((TILE, s_...  45.1 us
    pallas_call x1, Pallas kernels, source_call(): pl.pallas_call(body, grid=(wide // TILE,), in_specs=[part(0), part(1), pa...  22.9 us
    pallas_call x1, Pallas kernels, wall_part(): pl.pallas_call(kernel, grid=(steps,), in_specs=[pl.BlockSpec((group * TIL...  15.4 us
    ppermute x9, starting transfers between devices, send(): return lax.ppermute(x, ('span', 'plane'), pairs)  14.7 us
    pallas_call x1, Pallas kernels, bins_call(): pl.pallas_call(kernel, grid_spec=pltpu.PrefetchScalarGridSpec(num_scalar_...  11.7 us
    ppermute x9, waiting for transfers between devices, send(): return lax.ppermute(x, ('span', 'plane'), pairs)  8.14 us
    all_to_all x1, starting transfers between devices, local(): lax.all_to_all(tiles, ('span', 'plane'), split_axis=0, concat_axis=0, til...  3.69 us
  transfers between devices with their start and end apart: 10, of which 4 were waited for; matrix products, arithmetic and copies ran while one was open for 9% of the time, Pallas kernels for 52%

profile of v4, /device:TPU:0, one launch (start us, length us, event | category | flops | bytes accessed | tf_op | source)
XLA Modules:
  0.0 138.7 jit_solution(3853448373707708953)
XLA Ops:
  0.6 0.0 copy-start.1
  0.6 0.9 copy-done.1
  1.6 0.7 copy-done.2
  2.3 22.9 %source.1 = (f32[144,136,128]{2,1,0:T(8,128)S(1)}, f32[144,8,128]{2,1,0:T(8,128)S(1)}, f32[144,8,128]{2,1,0:T(8,128)S(1)}) custom-call(f32[3,128,128,128]{3,2,1,0:T(8,128)} %v.1, f32[3,128,128,128]{3,2,1,0:T(8,128)} %v.1, f32[3,128,128,128]{3,2,1,0:T(8,128)} %v.1, bf16[32,128]{1,0:T(8,128)(2,1)S(1)} %copy-done.2, bf16[768,128]{1,0:T(8,128)(2,1)S(1)} %copy-done.1), custom_call_target="tpu_custom_call" | custom-call | tf_op jit(solution)/shard_map/source/pallas_call | solution.py:185
  25.2 0.0 copy-start
  25.2 0.0 copy-done.3
  25.2 3.0 %collective-permute-start.2 = (s32[128]{0:T(128)S(1)}, s32[128]{0:T(128)S(1)}, u32[]{:S(2)}, u32[]{:S(2)}) collective-permute-start(s32[128]{0:T(128)S(1)} %copy-done.3), channel_id=1, source_target_pairs={{0,4},{1,5},{2,6},{3,7},{4,8},{5,9},{6,10},{7,11},{8,12},{9,13},{1... | collective-permute-start | bytes 1544 | tf_op jit(solution)/shard_map/ppermute | solution.py:559
  28.2 3.1 %collective-permute-start.3 = (s32[128]{0:T(128)S(1)}, s32[128]{0:T(128)S(1)}, u32[]{:S(2)}, u32[]{:S(2)}) collective-permute-start(s32[128]{0:T(128)S(1)} %copy-done.3), channel_id=1, source_target_pairs={{0,28},{1,29},{2,30},{3,31},{4,0},{5,1},{6,2},{7,3},{8,4},{9,5},{1... | collective-permute-start | bytes 1544 | tf_op jit(solution)/shard_map/ppermute | solution.py:559
  31.3 0.0 copy-done.10
  31.3 0.1 slice_convert_fusion.3
  31.4 0.0 copy-done
  31.4 0.1 fusion.35
  31.5 0.1 slice_select_fusion.3
  31.6 0.8 pad_maximum_fusion
  32.4 0.0 collective-permute-start
  32.4 0.8 pad_maximum_fusion.1
  33.2 1.7 %collective-permute-start.1 = (f32[6,152,128]{2,1,0:T(8,128)}, f32[6,152,128]{2,1,0:T(8,128)S(1)}, u32[]{:S(2)}, u32[]{:S(2)}) collective-permute-start(f32[6,152,128]{2,1,0:T(8,128)} %pad_maximum_fusion.1), channel_id=1, source_target_pairs={{0,3},{1,0},{2,1},{3,2},{4,7},{5,4},{6,5},{7,6},{8,11},{9,8},{10,9... | collective-permute-start | bytes 1400840 | tf_op jit(solution)/shard_map/ppermute | solution.py:559
  34.9 0.4 cosine_select_fusion.base
  35.3 0.0 copy-start.5
  35.3 0.0 copy-done.4
  35.3 0.6 slice.117
  35.9 11.7 %bins.2 = f32[2048,128]{1,0:T(8,128)S(1)} custom-call(s32[256]{0:T(256)S(1)} %copy-done.4, f32[255,128,128]{2,1,0:T(8,128)} %x.13, s32[1,128]{1,0:T(1,128)S(1)} %bitcast.13, f32[128,128]{1,0:T(8,128)S(1)} %slice.128.base), custom_call_target="tpu_custom_call" | custom-call | tf_op jit(solution)/shard_map/bins/pallas_call | solution.py:255
  47.7 0.7 compare_convert_fusion
  48.3 0.0 collective-permute-done
  48.4 0.0 copy-start.8
  48.4 0.1 fusion.37
  48.4 0.0 collective-permute-done.1
  48.5 0.1 fusion.38
  48.5 0.6 copy-done.8
  49.1 0.2 copy-done.9
  49.3 0.1 pad_add_fusion
  49.4 0.0 copy-done.5
  49.4 0.7 fusion.29
  50.1 0.7 fusion.28
  50.8 0.1 concatenate.18
  50.9 0.0 collective-permute-done.2
  50.9 0.0 collective-permute-done.3
  50.9 0.6 collective-permute-start.4
  51.5 4.2 %collective-permute-start.5 = (f32[144,8,128]{2,1,0:T(8,128)S(1)}, f32[144,8,128]{2,1,0:T(8,128)S(1)}, u32[]{:S(2)}, u32[]{:S(2)}) collective-permute-start(f32[144,8,128]{2,1,0:T(8,128)S(1)} %get-tuple-element.55), channel_id=1, source_target_pairs={{0,28},{1,29},{2,30},{3,31},{4,0},{5,1},{6,2},{7,3},{8,4},{9,5},{1... | collective-permute-start | bytes 1769480 | tf_op jit(solution)/shard_map/ppermute | solution.py:559
  55.6 0.5 broadcast_in_dim.155.station
  56.2 0.0 copy-done.11
  56.2 0.9 fusion.5.value
  57.0 15.4 %wall.1 = f32[32,128]{1,0:T(8,128)} custom-call(f32[144,136,128]{2,1,0:T(8,128)} %copy-done, bf16[768,1280]{1,0:T(8,128)(2,1)} %constant.168.clone.tab, s32[1,384]{1,0:T(1,128)} %broadcast_in_dim.155.station, f32[1,128]{1,0:T(1,128)} %constant.185.rate, f32[144,128]{1,0:T(8,128)} %fusion.5.value, f32[144,128]{1,0:T(8,128)} %copy-done.5), custom_call_target="tpu_custom_call" | custom-call | tf_op jit(solution)/shard_map/wall/pallas_call | solution.py:507
  72.5 1.9 %multiply_add_fusion = f32[32,64,128]{2,1,0:T(8,128)} fusion(f32[32,64,128]{2,1,0:T(8,128)S(1)} %bitcast.12, f32[32,128]{1,0:T(8,128)} %wall.1, f32[64]{0:T(128)S(1)} %compare_convert_fusion), kind=kLoop, calls=%fused_computation | loop fusion | flops 524288 | bytes 2113792 | tf_op jit(solution)/shard_map/add | solution.py:649
  74.4 2.4 %collective-permute-done.4.near = f32[144,8,128]{2,1,0:T(8,128)S(1)} collective-permute-done((f32[144,8,128]{2,1,0:T(8,128)S(1)}, f32[144,8,128]{2,1,0:T(8,128)S(1)}, u32[]{:S(2)}, u32[]{:S(2)}) %collective-permute-start.4) | collective-permute-done | bytes 589856 | tf_op jit(solution)/shard_map/ppermute | solution.py:559
  76.8 2.2 %collective-permute-done.5.far = f32[144,8,128]{2,1,0:T(8,128)S(1)} collective-permute-done((f32[144,8,128]{2,1,0:T(8,128)S(1)}, f32[144,8,128]{2,1,0:T(8,128)S(1)}, u32[]{:S(2)}, u32[]{:S(2)}) %collective-permute-start.5) | collective-permute-done | bytes 589856 | tf_op jit(solution)/shard_map/ppermute | solution.py:559
  79.0 3.7 %all-to-all-start = ((f32[32,64,128]{2,1,0:T(8,128)}), f32[32,64,128]{2,1,0:T(8,128)S(1)}, u32[]{:S(2)}, u32[]{:S(2)}) async-start(f32[32,64,128]{2,1,0:T(8,128)} %multiply_add_fusion), calls=%async_computation | async-start | bytes 2097152 | tf_op jit(solution)/shard_map/all_to_all | solution.py:659
  82.8 1.9 %fusion.1 = f32[144,136,128]{2,1,0:T(8,128)} fusion(f32[144,136,128]{2,1,0:T(8,128)} %copy-done, f32[6,152,128]{2,1,0:T(8,128)} %copy-done.8), kind=kLoop, calls=%fused_computation.8 | loop fusion | flops 104448 | bytes 1253376 | tf_op jit(solution)/shard_map/scatter-add | solution.py:652
  84.7 1.9 %fusion.s_in = f32[144,136,128]{2,1,0:T(8,128)} fusion(f32[144,136,128]{2,1,0:T(8,128)} %fusion.1, f32[6,152,128]{2,1,0:T(8,128)} %copy-done.9), kind=kLoop, calls=%fused_computation.6 | loop fusion | flops 104448 | bytes 1253376 | tf_op jit(solution)/shard_map/scatter-add | solution.py:653
  86.6 0.0 copy-done.6
  86.6 0.0 copy-done.7
  86.6 45.1 %project.1 = (f32[3,128,128,128]{3,2,1,0:T(8,128)}, f32[128,128,128]{2,1,0:T(8,128)}) custom-call(f32[144,136,128]{2,1,0:T(8,128)} %fusion.s_in, f32[144,8,128]{2,1,0:T(8,128)} %copy-done.6, f32[144,8,128]{2,1,0:T(8,128)} %copy-done.7, f32[3,128,128,128]{3,2,1,0:T(8,128)} %v.1, bf16[272,160]{1,0:T(8,128)(2,1)} %constant.171.clone.tab, ...), custom_call_target="tpu_custom_call" | custom-call | tf_op jit(solution)/shard_map/project/pallas_call | solution.py:378
  131.7 0.0 all-to-all-done
  131.7 0.1 reduce_sum.9
  131.8 0.3 fusion.10
  132.1 0.1 reshape.219
  132.2 1.6 %collective-permute-start.6 = (f32[1,8192]{1,0:T(1,128)S(1)}, f32[1,8192]{1,0:T(1,128)S(1)}, u32[]{:S(2)}, u32[]{:S(2)}) collective-permute-start(f32[1,8192]{1,0:T(1,128)S(1)} %reshape.219), channel_id=1, source_target_pairs={{0,3},{1,0},{2,1},{3,2},{4,7},{5,4},{6,5},{7,6},{8,11},{9,8},{10,9... | collective-permute-start | bytes 98312 | tf_op jit(solution)/shard_map/ppermute | solution.py:559
  133.8 0.4 collective-permute-start.7
  134.2 0.1 collective-permute-start.8
  134.3 0.1 broadcast_in_dim.169
  134.4 1.0 collective-permute-done.6
  135.4 2.5 %collective-permute-done.7 = f32[1,8192]{1,0:T(1,128)S(1)} collective-permute-done((f32[1,8192]{1,0:T(1,128)S(1)}, f32[1,8192]{1,0:T(1,128)S(1)}, u32[]{:S(2)}, u32[]{:S(2)}) %collective-permute-start.7) | collective-permute-done | bytes 32800 | tf_op jit(solution)/shard_map/ppermute | solution.py:559
  137.9 0.0 collective-permute-done.8
  137.9 0.8 select_select_fusion
  (24 shorter events, 0.1 us)
Async XLA Ops:
  0.6 0.9 copy-start.1
  1.6 0.7 copy-start.2
  2.3 23.0 %copy-start.3 = (s32[128]{0:T(128)S(1)}, s32[128]{0:T(128)}, u32[]{:S(2)}) copy-start(s32[128]{0:T(128)} %param.20) | copy-start | bytes 1540
  2.3 29.1 %copy-start.10 = (s32[128]{0:T(128)S(1)}, s32[128]{0:T(128)}, u32[]{:S(2)}) copy-start(s32[128]{0:T(128)} %param.21) | copy-start | bytes 1540
  2.3 33.1 %copy-start.4 = (s32[256]{0:T(256)S(1)}, s32[256]{0:T(256)}, u32[]{:S(2)}) copy-start(s32[256]{0:T(256)} %bins.3) | copy-start | bytes 3076
  25.2 6.2 %copy-start = (f32[144,136,128]{2,1,0:T(8,128)}, f32[144,136,128]{2,1,0:T(8,128)S(1)}, u32[]{:S(2)}) copy-start(f32[144,136,128]{2,1,0:T(8,128)S(1)} %get-tuple-element.61.s_in) | copy-start | bytes 30081028
  25.2 25.6 %collective-permute-start.2 = (s32[128]{0:T(128)S(1)}, s32[128]{0:T(128)S(1)}, u32[]{:S(2)}, u32[]{:S(2)}) collective-permute-start(s32[128]{0:T(128)S(1)} %copy-done.3), channel_id=1, source_target_pairs={{0,4},{1,5},{2,6},{3,7},{4,8},{5,9},{6,10},{7,11},{8,12},{9,13},{1... | collective-permute-start | bytes 1544 | tf_op jit(solution)/shard_map/ppermute | solution.py:559
  28.2 22.6 %collective-permute-start.3 = (s32[128]{0:T(128)S(1)}, s32[128]{0:T(128)S(1)}, u32[]{:S(2)}, u32[]{:S(2)}) collective-permute-start(s32[128]{0:T(128)S(1)} %copy-done.3), channel_id=1, source_target_pairs={{0,28},{1,29},{2,30},{3,31},{4,0},{5,1},{6,2},{7,3},{8,4},{9,5},{1... | collective-permute-start | bytes 1544 | tf_op jit(solution)/shard_map/ppermute | solution.py:559
  32.4 16.0 %collective-permute-start = (f32[6,152,128]{2,1,0:T(8,128)}, f32[6,152,128]{2,1,0:T(8,128)S(1)}, u32[]{:S(2)}, u32[]{:S(2)}) collective-permute-start(f32[6,152,128]{2,1,0:T(8,128)} %pad_maximum_fusion), channel_id=1, source_target_pairs={{0,1},{1,2},{2,3},{3,0},{4,5},{5,6},{6,7},{7,4},{8,9},{9,10},{10,1... | collective-permute-start | bytes 1400840 | tf_op jit(solution)/shard_map/ppermute | solution.py:559
  33.2 15.3 %collective-permute-start.1 = (f32[6,152,128]{2,1,0:T(8,128)}, f32[6,152,128]{2,1,0:T(8,128)S(1)}, u32[]{:S(2)}, u32[]{:S(2)}) collective-permute-start(f32[6,152,128]{2,1,0:T(8,128)} %pad_maximum_fusion.1), channel_id=1, source_target_pairs={{0,3},{1,0},{2,1},{3,2},{4,7},{5,4},{6,5},{7,6},{8,11},{9,8},{10,9... | collective-permute-start | bytes 1400840 | tf_op jit(solution)/shard_map/ppermute | solution.py:559
  35.3 14.1 %copy-start.5 = (f32[144,128]{1,0:T(8,128)}, f32[144,128]{1,0:T(8,128)S(1)}, u32[]{:S(2)}) copy-start(f32[144,128]{1,0:T(8,128)S(1)} %cosine_select_fusion.base) | copy-start | bytes 221188
  35.9 20.2 %copy-start.11 = (f32[8,128]{1,0:T(8,128)S(1)}, f32[8,128]{1,0:T(8,128)}, u32[]{:S(2)}) copy-start(f32[8,128]{1,0:T(8,128)} %constant.169.clone) | copy-start | bytes 12292
  48.4 0.8 copy-start.8
  48.4 0.8 copy-start.9
  50.9 25.9 %collective-permute-start.4 = (f32[144,8,128]{2,1,0:T(8,128)S(1)}, f32[144,8,128]{2,1,0:T(8,128)S(1)}, u32[]{:S(2)}, u32[]{:S(2)}) collective-permute-start(f32[144,8,128]{2,1,0:T(8,128)S(1)} %get-tuple-element.54), channel_id=1, source_target_pairs={{0,4},{1,5},{2,6},{3,7},{4,8},{5,9},{6,10},{7,11},{8,12},{9,13},{1... | collective-permute-start | bytes 1769480 | tf_op jit(solution)/shard_map/ppermute | solution.py:559
  51.5 27.5 %collective-permute-start.5 = (f32[144,8,128]{2,1,0:T(8,128)S(1)}, f32[144,8,128]{2,1,0:T(8,128)S(1)}, u32[]{:S(2)}, u32[]{:S(2)}) collective-permute-start(f32[144,8,128]{2,1,0:T(8,128)S(1)} %get-tuple-element.55), channel_id=1, source_target_pairs={{0,28},{1,29},{2,30},{3,31},{4,0},{5,1},{6,2},{7,3},{8,4},{9,5},{1... | collective-permute-start | bytes 1769480 | tf_op jit(solution)/shard_map/ppermute | solution.py:559
  76.8 9.8 %copy-start.6 = (f32[144,8,128]{2,1,0:T(8,128)}, f32[144,8,128]{2,1,0:T(8,128)S(1)}, u32[]{:S(2)}) copy-start(f32[144,8,128]{2,1,0:T(8,128)S(1)} %collective-permute-done.4.near) | copy-start | bytes 1769476
  79.0 7.6 %copy-start.7 = (f32[144,8,128]{2,1,0:T(8,128)}, f32[144,8,128]{2,1,0:T(8,128)S(1)}, u32[]{:S(2)}) copy-start(f32[144,8,128]{2,1,0:T(8,128)S(1)} %collective-permute-done.5.far) | copy-start | bytes 1769476
  79.0 52.7 %all-to-all-start = ((f32[32,64,128]{2,1,0:T(8,128)}), f32[32,64,128]{2,1,0:T(8,128)S(1)}, u32[]{:S(2)}, u32[]{:S(2)}) async-start(f32[32,64,128]{2,1,0:T(8,128)} %multiply_add_fusion), calls=%async_computation | async-start | bytes 2097152 | tf_op jit(solution)/shard_map/all_to_all | solution.py:659
  132.2 3.2 %collective-permute-start.6 = (f32[1,8192]{1,0:T(1,128)S(1)}, f32[1,8192]{1,0:T(1,128)S(1)}, u32[]{:S(2)}, u32[]{:S(2)}) collective-permute-start(f32[1,8192]{1,0:T(1,128)S(1)} %reshape.219), channel_id=1, source_target_pairs={{0,3},{1,0},{2,1},{3,2},{4,7},{5,4},{6,5},{7,6},{8,11},{9,8},{10,9... | collective-permute-start | bytes 98312 | tf_op jit(solution)/shard_map/ppermute | solution.py:559
  133.8 4.1 %collective-permute-start.7 = (f32[1,8192]{1,0:T(1,128)S(1)}, f32[1,8192]{1,0:T(1,128)S(1)}, u32[]{:S(2)}, u32[]{:S(2)}) collective-permute-start(f32[1,8192]{1,0:T(1,128)S(1)} %reshape.219), channel_id=1, source_target_pairs={{0,2},{1,3},{2,0},{3,1},{4,6},{5,7},{6,4},{7,5},{8,10},{9,11},{10,... | collective-permute-start | bytes 98312 | tf_op jit(solution)/shard_map/ppermute | solution.py:559
  134.2 3.7 %collective-permute-start.8 = (f32[1,8192]{1,0:T(1,128)S(1)}, f32[1,8192]{1,0:T(1,128)S(1)}, u32[]{:S(2)}, u32[]{:S(2)}) collective-permute-start(f32[1,8192]{1,0:T(1,128)S(1)} %reshape.219), channel_id=1, source_target_pairs={{0,1},{1,2},{2,3},{3,0},{4,5},{5,6},{6,7},{7,4},{8,9},{9,10},{10,1... | collective-permute-start | bytes 98312 | tf_op jit(solution)/shard_map/ppermute | solution.py:559
